TPU v7x, 128 devices: a whole 4x4x4 slice. The times are simulated.
128 devices in a mesh: row: 16 (over y_lo, z, core), col: 8 (over x, y_hi).
Axes of the slice: x: 4, y: 4 (y_hi: 2, y_lo: 2; y = y_hi * 2 + y_lo), z: 4, core: 2. Of those that a mesh axis runs over, the one named last changes fastest.
Arguments:
- coarse_kernel: bfloat16 [2048, 128, 128], P(('row', 'col')), may hold values from -6 to 6
- interp_index: int32 [16384, 4], P(('row', 'col')), may hold values from 0 to 2047, as said below
- interp_weight: float32 [16384, 4], P(('row', 'col')), may hold values from 0.2 to 1
- left_rot: bfloat16 [16384, 128, 128], P(('row', 'col')), may hold values from -0.5 to 0.5
- right_rot: bfloat16 [16384, 128, 128], P(('row', 'col')), may hold values from -0.5 to 0.5
- trial: bfloat16 [16384, 2048], P('col'), may hold values from -0.046875 to 0.046875
Outputs:
- product: float32 [16384, 2048], P('row', 'col')
Inputs may be any that keep to these rules, and one draw needn't show every extreme that they name: `interp_index`: within each aligned run of 128 fine blocks (the rows of one device), the entries name at most 2 different coarse blocks from any aligned group of 16 coarse blocks, and exactly 2 from at least one group.
All inputs are finite; a program needn't handle non-finite values.
Results may differ from a plain program's by a relative error of at most 0.0029.
Values may be sent and summed in bfloat16 or wider, within the bound.
No kernel may reach another device: no remote copies, remote signals or barrier semaphores. Data moves between devices by JAX's collectives and lax.ppermute only.
A program may use at most 128 MiB of HBM per device.

v0:
```python
import jax
import jax.numpy as jnp
from jax import lax
from jax.sharding import PartitionSpec as P

TC = 16
CAP = 2


def shards(coarse_kernel, interp_index, interp_weight, left_rot, right_rot, trial):
    row_count = lax.axis_size("row")
    col_count = lax.axis_size("col")
    dev_count = row_count * col_count
    coarse_per = coarse_kernel.shape[0]
    block_size = coarse_kernel.shape[1]
    blocks = interp_index.shape[0]
    ref_ids = interp_index.reshape(-1)
    catalog = jnp.arange(dev_count * coarse_per, dtype=jnp.int32)
    needed = (
        jnp.any(ref_ids[:, None] == catalog[None, :], axis=0)
        .astype(jnp.int32)
        .reshape(dev_count, coarse_per)
    )
    slot_rank = jnp.cumsum(needed, axis=1) - needed
    picker = needed[:, :, None] * (
        slot_rank[:, :, None] == jnp.arange(CAP, dtype=jnp.int32)[None, None, :]
    ).astype(jnp.int32)
    wanted = jnp.sum(picker * jnp.arange(coarse_per, dtype=jnp.int32)[None, :, None], axis=1)
    requested = lax.all_to_all(wanted, ("row", "col"), split_axis=0, concat_axis=0, tiled=True)
    served = jnp.take(coarse_kernel, requested.reshape(-1), axis=0).reshape(
        dev_count, CAP, block_size, block_size
    )
    arrived = lax.all_to_all(served, ("row", "col"), split_axis=0, concat_axis=0, tiled=True)
    arrived = arrived.reshape(dev_count * CAP, block_size, block_size)
    slot_table = (jnp.arange(dev_count, dtype=jnp.int32)[:, None] * CAP + slot_rank).reshape(-1)
    ref_slots = jnp.take(slot_table, ref_ids)
    picked = jnp.take(arrived, ref_slots, axis=0).reshape(blocks, 4, block_size, block_size)
    merged = jnp.sum(interp_weight[:, :, None, None] * picked.astype(jnp.float32), axis=1)
    turned = jnp.einsum(
        "fab,fbc->fac", left_rot.astype(jnp.float32), merged, precision=lax.Precision.HIGHEST
    )
    fine_blocks = jnp.einsum(
        "fac,fdc->fad", turned, right_rot.astype(jnp.float32), precision=lax.Precision.HIGHEST
    ).astype(jnp.bfloat16)
    gridded = lax.all_to_all(fine_blocks, ("row", "col"), split_axis=0, concat_axis=0, tiled=True)
    tile = gridded.reshape(blocks // TC, TC, block_size, block_size)
    vectors = trial.reshape(TC, block_size, trial.shape[1])
    partial_product = jnp.einsum("abxy,byv->axv", tile, vectors, preferred_element_type=jnp.float32)
    partial_product = partial_product.reshape(-1, trial.shape[1])
    return lax.psum_scatter(partial_product, "col", scatter_dimension=1, tiled=True)


def solution(mesh):
    return jax.shard_map(
        shards,
        mesh=mesh,
        in_specs=(
            P(("row", "col"), None, None),
            P(("row", "col"), None),
            P(("row", "col"), None),
            P(("row", "col"), None, None),
            P(("row", "col"), None, None),
            P("col", None),
        ),
        out_specs=P("row", "col"),
        check_vma=False,
    )
```

profile of v0, /device:TPU:0, one launch (start us, length us, event | category | flops | bytes accessed | tf_op | source)
XLA Modules:
  0.0 405.0 jit_solution(9256774075656323976)
XLA Ops:
  6.5 0.8 copy.71
  7.5 0.8 fusion
  8.5 0.1 copy.79
  8.6 20.4 %all_to_all.19 = s32[128,1,2]{2,1,0:T(1,128)S(1)} all-to-all(s32[128,1,2]{2,1,0:T(1,128)S(1)} %copy.79), channel_id=1, replica_groups=mesh['row'=16,'col'=8] {'row','col'}, dimensions={0} | all-to-all | bytes 2048 | tf_op jit(solution)/shard_map/all_to_all | solution.py:29
  29.0 0.5 broadcast.155
  29.5 0.8 reduce.3
  30.3 0.1 reshape.171
  30.5 8.5 %gather_fusion.1 = bf16[256,128,128]{2,1,0:T(8,128)(2,1)} fusion(bf16[16,128,128]{2,1,0:T(8,128)(2,1)S(1)} %copy-done, s32[1024]{0:T(1024)S(1)} %pad_clamp_fusion.1), kind=kCustom, calls=%fused_computation.1 | custom fusion | bytes 16778240 | tf_op jit(solution)/shard_map/jit(_take)/gather | solution.py:30
  39.0 7.4 %broadcast_select_fusion = bf16[128,2,128,128]{3,2,1,0:T(8,128)(2,1)} fusion(bf16[128,2,128,128]{3,2,1,0:T(8,128)(2,1)} %bitcast.23, pred[128,2]{1,0:T(8,128)(4,1)S(1)} %compare_and_fusion), kind=kLoop, calls=%fused_computation.4 | loop fusion | flops 4194304 | bytes 16777472 | tf_op jit(solution)/shard_map/jit(_take)/select_n | solution.py:30
  46.4 6.1 %all-to-all-start.1 = ((bf16[128,2,128,128]{3,2,1,0:T(8,128)(2,1)}), bf16[128,2,128,128]{3,2,1,0:T(8,128)(2,1)}, u32[]{:S(2)}, u32[]{:S(2)}) async-start(bf16[128,2,128,128]{3,2,1,0:T(8,128)(2,1)} %broadcast_select_fusion), calls=%async_computation.1 | async-start | bytes 16777216 | tf_op jit(solution)/shard_map/all_to_all | solution.py:33
  52.5 0.2 reduce-scatter.2.cloned.1.call-start
  53.2 3.1 gather_fusion
  56.6 0.1 copy.76
  56.7 0.1 copy.70
  56.9 102.7 %all-to-all-done.1 = bf16[128,2,128,128]{3,2,1,0:T(8,128)(2,1)} async-done(((bf16[128,2,128,128]{3,2,1,0:T(8,128)(2,1)}), bf16[128,2,128,128]{3,2,1,0:T(8,128)(2,1)}, u32[]{:S(2)}, u32[]{:S(2)}) %all-to-all-start.1) | async-done | bytes 8388640 | tf_op jit(solution)/shard_map/all_to_all | solution.py:33
  159.6 17.3 %gather_fusion.2 = bf16[512,128,128]{2,1,0:T(8,128)(2,1)} fusion(bf16[256,128,128]{2,1,0:T(8,128)(2,1)} %bitcast.5, s32[1024]{0:T(1024)S(1)} %pad_clamp_fusion), kind=kCustom, calls=%fused_computation.2 | custom fusion | bytes 33556480 | tf_op jit(solution)/shard_map/jit(_take)/gather | solution.py:37
  176.8 11.3 %multiply_reduce_fusion = f32[128,128,128]{2,1,0:T(8,128)S(1)} fusion(f32[128,4]{1,0:T(8,128)S(1)} %copy.70, pred[128,4]{1,0:T(8,128)(4,1)S(1)} %copy.76, bf16[512,128,128]{2,1,0:T(8,128)(2,1)} %gather_fusion.2), kind=kLoop, calls=%fused_computation.3 | loop fusion | flops 31457280 | bytes 25168384 | tf_op jit(solution)/shard_map/reduce_sum | solution.py:38
  188.1 8.5 %fusion.1 = f32[128,128,128]{1,2,0:T(8,128)} fusion(f32[128,128,128]{2,1,0:T(8,128)S(1)} %multiply_reduce_fusion, bf16[128,128,128]{2,1,0:T(8,128)(2,1)} %param.9), kind=kOutput, calls=%fused_computation.25 | convolution fusion | flops 3221225472 | bytes 20971520 | tf_op jit(solution)/shard_map/fab,fbc->fac/dot_general | solution.py:39
  196.7 13.3 %convolution_convert_fusion = bf16[128,128,128]{2,1,0:T(8,128)(2,1)S(1)} fusion(f32[128,128,128]{1,2,0:T(8,128)} %fusion.1, bf16[128,128,128]{2,1,0:T(8,128)(2,1)} %param.10), kind=kOutput, calls=%fused_computation.8 | convolution fusion | flops 3223322624 | bytes 16777216 | tf_op jit(solution)/shard_map/fac,fdc->fad/dot_general | solution.py:42
  210.0 64.0 %all_to_all.20 = bf16[128,128,128]{2,1,0:T(8,128)(2,1)S(1)} all-to-all(bf16[128,128,128]{2,1,0:T(8,128)(2,1)S(1)} %convolution_convert_fusion), channel_id=1, replica_groups=mesh['row'=16,'col'=8] {'row','col'}, dimensions={0} | all-to-all | bytes 8388608 | tf_op jit(solution)/shard_map/all_to_all | solution.py:45
  274.0 0.6 copy.82
  274.6 1.6 slice-done.1
  276.2 10.9 %convolution_bitcast_fusion = f32[1024,2048]{1,0:T(8,128)} fusion(bf16[1024,16,128]{2,0,1:T(8,128)(2,1)S(1)} %bitcast.25, bf16[16,128,2048]{2,1,0:T(8,128)(2,1)S(1)} %bitcast.34), kind=kOutput, calls=%fused_computation.5 | convolution fusion | flops 8589934592 | bytes 20971520 | tf_op jit(solution)/shard_map/abxy,byv->axv/dot_general | solution.py:48
  287.1 111.0 %reduce-scatter.2.cloned.1.call-done = f32[1024,256]{1,0:T(8,128)} async-done(((f32[1024,2048]{1,0:T(8,128)}), f32[1024,256]{1,0:T(8,128)}) %reduce-scatter.2.cloned.1.call-update) | async-done | bytes 1048592 | tf_op jit(solution)/shard_map/reduce_scatter | solution.py:50
  (37 shorter events, 1.1 us)
Async XLA Ops:
  6.5 24.0 %copy-start = (bf16[16,128,128]{2,1,0:T(8,128)(2,1)S(1)}, bf16[16,128,128]{2,1,0:T(8,128)(2,1)}, u32[]{:S(2)}) copy-start(bf16[16,128,128]{2,1,0:T(8,128)(2,1)} %param.6) | copy-start | bytes 1572868
  46.4 10.1 %copy-start.2 = (s32[128,4]{0,1:T(4,128)S(1)}, s32[128,4]{0,1:T(4,128)}, u32[]{:S(2)}) copy-start(s32[128,4]{0,1:T(4,128)} %param.7) | copy-start | bytes 6148
  46.4 10.3 %copy-start.3 = (f32[128,4]{0,1:T(4,128)S(1)}, f32[128,4]{0,1:T(4,128)}, u32[]{:S(2)}) copy-start(f32[128,4]{0,1:T(4,128)} %param.8) | copy-start | bytes 6148
  46.4 113.1 %all-to-all-start.1 = ((bf16[128,2,128,128]{3,2,1,0:T(8,128)(2,1)}), bf16[128,2,128,128]{3,2,1,0:T(8,128)(2,1)}, u32[]{:S(2)}, u32[]{:S(2)}) async-start(bf16[128,2,128,128]{3,2,1,0:T(8,128)(2,1)} %broadcast_select_fusion), calls=%async_computation.1 | async-start | bytes 16777216 | tf_op jit(solution)/shard_map/all_to_all | solution.py:33
  52.5 345.6 %reduce-scatter.2.cloned.1.call-start = ((), (), s32[]{:S(2)}) async-start(), calls=%async_computation.4 | async-start | bytes 9437184 | tf_op jit(solution)/shard_map/reduce_scatter | solution.py:50
  210.0 64.6 %slice-start = ((s8[8388608]{0:T(1024)(128)(4,1)}), s8[4194304]{0:T(1024)(128)(4,1)S(1)}, s32[]{:S(2)}) async-start(s8[8388608]{0:T(1024)(128)(4,1)} %bitcast.32), calls=%async_computation.5 | async-start | bytes 8388608
  274.0 2.2 slice-start.1
  276.2 122.0 %copy-start.1 = (bf16[16,128,128]{2,1,0:T(8,128)(2,1)S(1)}, bf16[16,128,128]{2,1,0:T(8,128)(2,1)}, u32[]{:S(2)}) copy-start(bf16[16,128,128]{2,1,0:T(8,128)(2,1)} %param.6) | copy-start | bytes 1572868
Sparse Core Ops, SparseCore 0:
  287.3 110.8 reduce-scatter.1
where the time goes:
time: 405 us
  waiting for transfers between devices  214 us (53%)
  blocking collectives  84.4 us (21%)
  local copies, waits for them, and re-layouts  33.8 us (8%)
  matrix products  32.7 us (8%)
  other arithmetic  20.5 us (5%)
  between operations  13.6 us (3%)
  starting transfers between devices  6.28 us (2%)
    reduce_scatter x1, waiting for transfers between devices, shards(): lax.psum_scatter(partial_product, 'col', scatter_dimension=1, tiled=True)  111 us
    all_to_all x1, waiting for transfers between devices, shards(): lax.all_to_all(served, ('row', 'col'), split_axis=0, concat_axis=0, tiled...  103 us
    all_to_all x1, blocking collectives, shards(): lax.all_to_all(fine_blocks, ('row', 'col'), split_axis=0, concat_axis=0,...  64 us
    all_to_all x1, blocking collectives, shards(): lax.all_to_all(wanted, ('row', 'col'), split_axis=0, concat_axis=0, tiled...  20.4 us
    gather x1, local copies, waits for them, and re-layouts, shards(): jnp.take(arrived, ref_slots, axis=0)  17.3 us
    dot_general x1, matrix products, shards(): jnp.einsum('fac,fdc->fad', turned, right_rot.astype(jnp.float32), precisi...  13.3 us
    reduce_sum x1, other arithmetic, shards(): jnp.sum(interp_weight[:, :, None, None] * picked.astype(jnp.float32), axi...  11.3 us
    dot_general x1, matrix products, shards(): jnp.einsum('abxy,byv->axv', tile, vectors, preferred_element_type=jnp.flo...  10.9 us
  transfers between devices with their start and end apart: 2, of which 2 were waited for; matrix products, arithmetic and copies ran while one was open for 1% of the time, Pallas kernels for 0%

commit v1 on v0

v1 whole, which is shorter than its diff:
```python
import jax
import jax.numpy as jnp
from jax import lax
from jax.experimental import pallas as pl
from jax.experimental.pallas import tpu as pltpu
from jax.sharding import PartitionSpec as P

TC = 16
CAP = 2
STEP = 8


def serve_kernel(wanted, coarse, out, sem):
    count = out.shape[0]

    def issue(i, carry):
        pltpu.make_async_copy(coarse.at[wanted[i]], out.at[i], sem).start()
        return carry

    lax.fori_loop(0, count, issue, 0, unroll=8)
    pltpu.make_async_copy(out, out, sem).wait()


def serve(wanted, coarse_kernel):
    count = wanted.shape[0]
    return pl.pallas_call(
        serve_kernel,
        grid_spec=pltpu.PrefetchScalarGridSpec(
            num_scalar_prefetch=1,
            grid=(),
            in_specs=[pl.BlockSpec(memory_space=pltpu.VMEM)],
            out_specs=pl.BlockSpec(memory_space=pl.ANY),
            scratch_shapes=[pltpu.SemaphoreType.DMA],
        ),
        out_shape=jax.ShapeDtypeStruct((count,) + coarse_kernel.shape[1:], coarse_kernel.dtype),
        name="serve",
    )(wanted, coarse_kernel)


def split(value):
    high = value.astype(jnp.bfloat16)
    low = (value - high.astype(jnp.float32)).astype(jnp.bfloat16)
    return high, low


def rotate_kernel(slots, weights, arrived, left, right, out):
    base = pl.program_id(0) * left.shape[0]
    for k in range(left.shape[0]):
        f = (base + k) * 4
        merged = weights[f] * arrived[slots[f]].astype(jnp.float32)
        for j in range(1, 4):
            merged += weights[f + j] * arrived[slots[f + j]].astype(jnp.float32)
        lhs = left[k]
        turned = jnp.dot(
            jnp.concatenate([lhs, lhs], axis=1),
            jnp.concatenate(split(merged), axis=0),
            preferred_element_type=jnp.float32,
        )
        rhs = right[k]
        fine = lax.dot_general(
            jnp.concatenate(split(turned), axis=1),
            jnp.concatenate([rhs, rhs], axis=1),
            (((1,), (1,)), ((), ())),
            preferred_element_type=jnp.float32,
        )
        out[k] = fine.astype(jnp.bfloat16)


def rotate(slots, weights, arrived, left, right):
    blocks, size, _ = left.shape
    spec = pl.BlockSpec((STEP, size, size), lambda i, *_: (i, 0, 0))
    return pl.pallas_call(
        rotate_kernel,
        grid_spec=pltpu.PrefetchScalarGridSpec(
            num_scalar_prefetch=2,
            grid=(blocks // STEP,),
            in_specs=[pl.BlockSpec(memory_space=pltpu.VMEM), spec, spec],
            out_specs=spec,
        ),
        out_shape=jax.ShapeDtypeStruct(left.shape, jnp.bfloat16),
        name="rotate",
    )(slots, weights, arrived, left, right)


def panel_kernel(tile, vectors, out):
    parts, _, width = out.shape
    lhs = jnp.concatenate([tile[b] for b in range(TC)], axis=1)
    for part in range(parts):
        out[part] = jnp.dot(
            lhs, vectors[:, part * width : (part + 1) * width], preferred_element_type=jnp.float32
        ).astype(jnp.bfloat16)


def panel_product(gridded, trial, parts):
    blocks, size, _ = gridded.shape
    width = trial.shape[1] // parts
    rows = blocks // TC
    return pl.pallas_call(
        panel_kernel,
        grid=(rows,),
        in_specs=[
            pl.BlockSpec((TC, size, size), lambda a: (a, 0, 0)),
            pl.BlockSpec(memory_space=pltpu.VMEM),
        ],
        out_specs=pl.BlockSpec((parts, size, width), lambda a: (0, a, 0)),
        out_shape=jax.ShapeDtypeStruct((parts, rows * size, width), jnp.bfloat16),
        name="panel",
    )(gridded, trial)


def shards(coarse_kernel, interp_index, interp_weight, left_rot, right_rot, trial):
    col_count = lax.axis_size("col")
    dev_count = lax.axis_size("row") * col_count
    coarse_per = coarse_kernel.shape[0]
    ref_ids = interp_index.reshape(-1)
    catalog = jnp.arange(dev_count * coarse_per, dtype=jnp.int32)
    needed = (
        jnp.any(ref_ids[:, None] == catalog[None, :], axis=0)
        .astype(jnp.int32)
        .reshape(dev_count, coarse_per)
    )
    slot_rank = jnp.cumsum(needed, axis=1) - needed
    picker = needed[:, :, None] * (
        slot_rank[:, :, None] == jnp.arange(CAP, dtype=jnp.int32)[None, None, :]
    ).astype(jnp.int32)
    wanted = jnp.sum(picker * jnp.arange(coarse_per, dtype=jnp.int32)[None, :, None], axis=1)
    requested = lax.all_to_all(wanted, ("row", "col"), split_axis=0, concat_axis=0, tiled=True)
    served = serve(requested.reshape(-1), coarse_kernel).reshape(
        (dev_count, CAP) + coarse_kernel.shape[1:]
    )
    arrived = lax.all_to_all(served, ("row", "col"), split_axis=0, concat_axis=0, tiled=True)
    arrived = arrived.reshape((dev_count * CAP,) + coarse_kernel.shape[1:])
    slot_table = (jnp.arange(dev_count, dtype=jnp.int32)[:, None] * CAP + slot_rank).reshape(-1)
    ref_slots = jnp.take(slot_table, ref_ids, mode="clip")
    fine_blocks = rotate(ref_slots, interp_weight.reshape(-1), arrived, left_rot, right_rot)
    gridded = lax.all_to_all(fine_blocks, ("row", "col"), split_axis=0, concat_axis=0, tiled=True)
    partial_product = panel_product(gridded, trial, col_count)
    shares = lax.all_to_all(partial_product, "col", split_axis=0, concat_axis=0, tiled=True)
    return jnp.sum(shares.astype(jnp.float32), axis=0)


def solution(mesh):
    return jax.shard_map(
        shards,
        mesh=mesh,
        in_specs=(
            P(("row", "col"), None, None),
            P(("row", "col"), None),
            P(("row", "col"), None),
            P(("row", "col"), None, None),
            P(("row", "col"), None, None),
            P("col", None),
        ),
        out_specs=P("row", "col"),
        check_vma=False,
    )
```

time: 405 us -> 296 us (0.73)
  waiting for transfers between devices: 214 us -> 102 us
  blocking collectives: 84.4 us -> 139 us
  Pallas kernels: 0 us -> 37.9 us
  matrix products: 32.7 us -> 0 us
  local copies, waits for them, and re-layouts: 33.8 us -> 7.79 us
  other arithmetic: 20.5 us -> 3.2 us
  between operations: 13.6 us -> 0.08 us
    reduce_scatter x1 -> x0, waiting for transfers between devices: 111 us -> none  [shards(): lax.psum_scatter(partial_product, 'col', scatter_dimension=1, tiled=True)]
    all_to_all x0 -> x1, blocking collectives: none -> 54.4 us  [shards(): lax.all_to_all(partial_product, 'col', split_axis=0, concat_axis=0, tiled...]
    pallas_call x0 -> x3, Pallas kernels: none -> 37.9 us  [the longest x1 18.3 us: rotate(): pl.pallas_call(rotate_kernel, grid_spec=pltpu.PrefetchScalarGridSpec(num_...]
    dot_general x3 -> x0, matrix products: 32.7 us -> none  [the longest x1 13.3 us: shards(): jnp.einsum('fac,fdc->fad', turned, right_rot.astype(jnp.float32), precisi...]
    gather x5 -> x1, local copies, waits for them, and re-layouts: 29.1 us -> 4.28 us  [shards(): ref_slots = jnp.take(slot_table, ref_ids, mode='clip')]
    reduce_sum x1, other arithmetic: 11.3 us -> 1.55 us  [shards(): return jnp.sum(shares.astype(jnp.float32), axis=0)]
    select_n x4 -> x0, other arithmetic: 7.45 us -> none  [the longest x2 7.44 us: shards(): jnp.take(coarse_kernel, requested.reshape(-1), axis=0)]
  transfers between devices with their start and end apart: 2 -> 1, of which waited for: 2 -> 1; matrix products, arithmetic and copies ran while one was open for 1% -> 2% of each run, Pallas kernels for 0% -> 0%
where the time goes in v1:
time: 296 us
  blocking collectives  139 us (47%)
  waiting for transfers between devices  102 us (34%)
  Pallas kernels  37.9 us (13%)
  local copies, waits for them, and re-layouts  7.79 us (3%)
  starting transfers between devices  5.94 us (2%)
  other arithmetic  3.2 us (1%)
    all_to_all x1, waiting for transfers between devices, shards(): lax.all_to_all(served, ('row', 'col'), split_axis=0, concat_axis=0, tiled...  102 us
    all_to_all x1, blocking collectives, shards(): lax.all_to_all(fine_blocks, ('row', 'col'), split_axis=0, concat_axis=0,...  64.3 us
    all_to_all x1, blocking collectives, shards(): lax.all_to_all(partial_product, 'col', split_axis=0, concat_axis=0, tiled...  54.4 us
    all_to_all x1, blocking collectives, shards(): lax.all_to_all(wanted, ('row', 'col'), split_axis=0, concat_axis=0, tiled...  20.4 us
    pallas_call x1, Pallas kernels, rotate(): pl.pallas_call(rotate_kernel, grid_spec=pltpu.PrefetchScalarGridSpec(num_...  18.3 us
    pallas_call x1, Pallas kernels, panel_product(): pl.pallas_call(panel_kernel, grid=(rows,), in_specs=[pl.BlockSpec((TC, si...  14.7 us
    all_to_all x1, starting transfers between devices, shards(): lax.all_to_all(served, ('row', 'col'), split_axis=0, concat_axis=0, tiled...  5.94 us
  transfers between devices with their start and end apart: 1, of which 1 were waited for; matrix products, arithmetic and copies ran while one was open for 2% of the time, Pallas kernels for 0%

profile of v1, /device:TPU:0, one launch (start us, length us, event | category | flops | bytes accessed | tf_op | source)
XLA Modules:
  0.0 295.6 jit_solution(3457949481142226059)
XLA Ops:
  0.0 0.8 copy.21
  0.8 0.1 eq.28
  0.9 0.8 fusion
  1.7 0.1 reshape.45
  1.9 0.1 copy.27
  2.0 20.4 %all_to_all.24 = s32[128,1,2]{2,1,0:T(1,128)S(1)} all-to-all(s32[128,1,2]{2,1,0:T(1,128)S(1)} %copy.27), channel_id=1, replica_groups=mesh['row'=16,'col'=8] {'row','col'}, dimensions={0} | all-to-all | bytes 2048 | tf_op jit(solution)/shard_map/all_to_all | solution.py:127
  22.4 0.5 broadcast.18
  22.9 0.8 reduce.3
  23.7 0.7 reshape.42.wanted
  24.4 4.9 %serve.1 = bf16[256,128,128]{2,1,0:T(8,128)(2,1)} custom-call(s32[256]{0:T(256)} %reshape.42.wanted, bf16[16,128,128]{2,1,0:T(8,128)(2,1)} %coarse.1), custom_call_target="tpu_custom_call" | custom-call | tf_op jit(solution)/shard_map/serve/pallas_call | solution.py:26
  29.4 5.9 %all-to-all-start.1 = ((bf16[128,2,128,128]{3,2,1,0:T(8,128)(2,1)}), bf16[128,2,128,128]{3,2,1,0:T(8,128)(2,1)}, u32[]{:S(2)}, u32[]{:S(2)}) async-start(bf16[128,2,128,128]{3,2,1,0:T(8,128)(2,1)} %bitcast.3), calls=%async_computation.1 | async-start | bytes 16777216 | tf_op jit(solution)/shard_map/all_to_all | solution.py:131
  35.3 0.1 copy.23
  35.5 0.1 add.11
  35.5 0.1 add.12
  35.6 0.1 reduce_window_sum.14
  35.7 0.1 copy.24
  35.8 0.7 reshape.41.weights
  36.5 4.3 %gather_fusion = s32[512]{0:T(512)} fusion(s32[2048]{0:T(1024)S(1)} %subtract_add_fusion, s32[1024]{0:T(1024)S(1)} %pad_clamp_fusion), kind=kCustom, calls=%fused_computation | custom fusion | bytes 6144 | tf_op jit(solution)/shard_map/jit(_take)/gather | solution.py:134
  40.8 101.6 %all-to-all-done.1 = bf16[128,2,128,128]{3,2,1,0:T(8,128)(2,1)} async-done(((bf16[128,2,128,128]{3,2,1,0:T(8,128)(2,1)}), bf16[128,2,128,128]{3,2,1,0:T(8,128)(2,1)}, u32[]{:S(2)}, u32[]{:S(2)}) %all-to-all-start.1) | async-done | bytes 8388640 | tf_op jit(solution)/shard_map/all_to_all | solution.py:131
  142.4 18.3 %rotate.1 = bf16[128,128,128]{2,1,0:T(8,128)(2,1)} custom-call(s32[512]{0:T(512)} %gather_fusion, f32[512]{0:T(512)} %reshape.41.weights, bf16[256,128,128]{2,1,0:T(8,128)(2,1)} %bitcast.2.arrived, bf16[128,128,128]{2,1,0:T(8,128)(2,1)} %left.1, bf16[128,128,128]{2,1,0:T(8,128)(2,1)} %right.1), custom_call_target="tpu_custom_call" | custom-call | tf_op jit(solution)/shard_map/rotate/pallas_call | solution.py:72
  160.7 64.3 %all_to_all.25.tile = bf16[128,128,128]{2,1,0:T(8,128)(2,1)} all-to-all(bf16[128,128,128]{2,1,0:T(8,128)(2,1)} %rotate.1), channel_id=1, replica_groups=mesh['row'=16,'col'=8] {'row','col'}, dimensions={0} | all-to-all | bytes 8388608 | tf_op jit(solution)/shard_map/all_to_all | solution.py:136
  225.0 14.7 %panel.1 = bf16[8,1024,256]{2,1,0:T(8,128)(2,1)} custom-call(bf16[128,128,128]{2,1,0:T(8,128)(2,1)} %all_to_all.25.tile, bf16[2048,2048]{1,0:T(8,128)(2,1)} %vectors.1), custom_call_target="tpu_custom_call" | custom-call | tf_op jit(solution)/shard_map/panel/pallas_call | solution.py:98
  239.7 54.4 %all_to_all.26 = bf16[8,1024,256]{2,1,0:T(8,128)(2,1)S(1)} all-to-all(bf16[8,1024,256]{2,1,0:T(8,128)(2,1)} %panel.1), channel_id=1, replica_groups=mesh['row'=16,'col'=8] {'col'}, dimensions={0} | all-to-all | bytes 8388608 | tf_op jit(solution)/shard_map/all_to_all | solution.py:138
  294.0 1.5 convert_reduce_fusion
  (10 shorter events, 0.2 us)
Async XLA Ops:
  29.4 6.3 %copy-start = (f32[128,4]{0,1:T(4,128)S(1)}, f32[128,4]{0,1:T(4,128)}, u32[]{:S(2)}) copy-start(f32[128,4]{0,1:T(4,128)} %param.8) | copy-start | bytes 6148
  29.4 113.0 %all-to-all-start.1 = ((bf16[128,2,128,128]{3,2,1,0:T(8,128)(2,1)}), bf16[128,2,128,128]{3,2,1,0:T(8,128)(2,1)}, u32[]{:S(2)}, u32[]{:S(2)}) async-start(bf16[128,2,128,128]{3,2,1,0:T(8,128)(2,1)} %bitcast.3), calls=%async_computation.1 | async-start | bytes 16777216 | tf_op jit(solution)/shard_map/all_to_all | solution.py:131

commit v2 on v1

v2 whole, which is shorter than its diff:
```python
import functools

import jax
import jax.numpy as jnp
from jax import lax
from jax.experimental import pallas as pl
from jax.experimental.pallas import tpu as pltpu
from jax.sharding import Mesh, PartitionSpec as P

CAP = 2
UNROLL = 16
CHUNKS = 4
ALL = ("ylo", "z", "core", "x", "yhi")
COL = ("x", "yhi")
SAME_CORE = ("ylo", "z", "x", "yhi")


def serve_kernel(wanted, coarse, out, sem):
    def issue(i, carry):
        pltpu.make_async_copy(coarse.at[wanted[i]], out.at[i], sem).start()
        return carry

    lax.fori_loop(0, out.shape[0], issue, 0, unroll=8)
    pltpu.make_async_copy(out, out, sem).wait()


def serve(wanted, coarse_kernel):
    count = wanted.shape[0]
    return pl.pallas_call(
        serve_kernel,
        grid_spec=pltpu.PrefetchScalarGridSpec(
            num_scalar_prefetch=1,
            grid=(),
            in_specs=[pl.BlockSpec(memory_space=pltpu.VMEM)],
            out_specs=pl.BlockSpec(memory_space=pl.ANY),
            scratch_shapes=[pltpu.SemaphoreType.DMA],
        ),
        out_shape=jax.ShapeDtypeStruct((count,) + coarse_kernel.shape[1:], coarse_kernel.dtype),
        name="serve",
    )(wanted, coarse_kernel)


def split(value):
    high = value.astype(jnp.bfloat16)
    low = (value - high.astype(jnp.float32)).astype(jnp.bfloat16)
    return high, low


def rotate_kernel(
    core, slots, weights, arrived, left, right, mine, theirs,
    arrived_v, left_v, right_v, out_v, sem_arrived, sem_left, sem_right, sem_mine, sem_theirs,
):
    blocks = left.shape[0]
    span = blocks // CHUNKS
    groups = mine.shape[0] // 8
    copies = []
    first = pltpu.make_async_copy(arrived, arrived_v, sem_arrived)
    first.start()
    for n in range(CHUNKS):
        part = pl.ds(n * span, span)
        pair = (
            pltpu.make_async_copy(left.at[part], left_v.at[part], sem_left.at[n]),
            pltpu.make_async_copy(right.at[part], right_v.at[part], sem_right.at[n]),
        )
        for copy in pair:
            copy.start()
        copies.append(pair)
    first.wait()

    def block(f):
        r = f * 4
        merged = weights[r] * arrived_v[slots[r]].astype(jnp.float32)
        for j in range(1, 4):
            merged += weights[r + j] * arrived_v[slots[r + j]].astype(jnp.float32)
        lhs = left_v[f]
        turned = jnp.dot(
            jnp.concatenate([lhs, lhs], axis=1),
            jnp.concatenate(split(merged), axis=0),
            preferred_element_type=jnp.float32,
        )
        rhs = right_v[f]
        fine = lax.dot_general(
            jnp.concatenate(split(turned), axis=1),
            jnp.concatenate([rhs, rhs], axis=1),
            (((1,), (1,)), ((), ())),
            preferred_element_type=jnp.float32,
        )
        out_v[f] = fine.astype(jnp.bfloat16)

    for n in range(CHUNKS):
        for copy in copies[n]:
            copy.wait()

        def several(i, carry):
            for k in range(UNROLL):
                block(n * span + i * UNROLL + k)
            return carry

        lax.fori_loop(0, span // UNROLL, several, 0)
        for g in range(n * groups // CHUNKS, (n + 1) * groups // CHUNKS):
            pltpu.make_async_copy(
                out_v.at[pl.ds(g * 16 + core[0] * 8, 8)], mine.at[pl.ds(g * 8, 8)], sem_mine
            ).start()
            pltpu.make_async_copy(
                out_v.at[pl.ds(g * 16 + (1 - core[0]) * 8, 8)], theirs.at[pl.ds(g * 8, 8)], sem_theirs
            ).start()
    pltpu.make_async_copy(mine, mine, sem_mine).wait()
    pltpu.make_async_copy(theirs, theirs, sem_theirs).wait()


def rotate(core, slots, weights, arrived, left, right):
    half = jax.ShapeDtypeStruct((left.shape[0] // 2,) + left.shape[1:], jnp.bfloat16)
    anywhere = pl.BlockSpec(memory_space=pl.ANY)
    return pl.pallas_call(
        rotate_kernel,
        grid_spec=pltpu.PrefetchScalarGridSpec(
            num_scalar_prefetch=3,
            grid=(),
            in_specs=[anywhere] * 3,
            out_specs=[anywhere] * 2,
            scratch_shapes=[
                pltpu.VMEM(arrived.shape, jnp.bfloat16),
                pltpu.VMEM(left.shape, jnp.bfloat16),
                pltpu.VMEM(left.shape, jnp.bfloat16),
                pltpu.VMEM(left.shape, jnp.bfloat16),
                pltpu.SemaphoreType.DMA,
                pltpu.SemaphoreType.DMA((CHUNKS,)),
                pltpu.SemaphoreType.DMA((CHUNKS,)),
                pltpu.SemaphoreType.DMA,
                pltpu.SemaphoreType.DMA,
            ],
        ),
        out_shape=[half, half],
        name="rotate",
    )(core, slots, weights, arrived, left, right)


def panel_kernel(place, mine, other, *refs):
    pieces, rest = refs[:10], refs[10:]
    out, mine_v, other_v, vec_v, out_v, sem_rows, sem_vec, sem_out = rest
    copies = [
        pltpu.make_async_copy(mine, mine_v, sem_rows.at[0]),
        pltpu.make_async_copy(other, other_v, sem_rows.at[1]),
    ]
    half = vec_v.shape[2] // 2
    vec_copies = []
    for side in range(2):
        own, before, after, top, bottom = pieces[side * 5 : side * 5 + 5]
        targets = (
            (own, vec_v.at[side, 0]),
            (after, vec_v.at[side, 1]),
            (top, vec_v.at[side, 2, pl.ds(0, half)]),
            (bottom, vec_v.at[side, 2, pl.ds(half, half)]),
            (before, vec_v.at[side, 3]),
        )
        vec_copies.append(
            [pltpu.make_async_copy(a, b, sem_vec.at[side, n]) for n, (a, b) in enumerate(targets)]
        )
    for copy in copies + vec_copies[0] + vec_copies[1]:
        copy.start()
    for copy in copies:
        copy.wait()
    groups = mine_v.shape[0] // 8
    for side in range(2):
        for copy in vec_copies[side]:
            copy.wait()
        order = (mine_v, other_v) if side == 0 else (other_v, mine_v)

        def part(rel, carry):
            lhs = jnp.concatenate(
                [
                    jnp.concatenate([order[q][g * 8 + c] for c in range(8) for q in range(2)], axis=1)
                    for g in range(groups)
                ],
                axis=0,
            )
            rhs = vec_v[side, rel].reshape(-1, vec_v.shape[-1])
            out_v[side * 4 + rel] = (
                jnp.dot(lhs, rhs, preferred_element_type=jnp.float32)
                .astype(jnp.bfloat16)
                .reshape(out_v.shape[1:])
            )
            core = place[1] if side == 0 else 1 - place[1]
            target = lax.rem(place[0] + rel, 4) * 2 + core
            pltpu.make_async_copy(out_v.at[side * 4 + rel], out.at[:, target], sem_out).start()
            return carry

        lax.fori_loop(0, 4, part, 0)
    pltpu.make_async_copy(out_v, out_v, sem_out).wait()


def panel_product(place, mine, other, pieces):
    groups = mine.shape[0] // 8
    size = mine.shape[1]
    width = pieces[0].shape[-1]
    anywhere = pl.BlockSpec(memory_space=pl.ANY)
    return pl.pallas_call(
        panel_kernel,
        grid_spec=pltpu.PrefetchScalarGridSpec(
            num_scalar_prefetch=1,
            grid=(),
            in_specs=[anywhere] * 12,
            out_specs=anywhere,
            scratch_shapes=[
                pltpu.VMEM(mine.shape, jnp.bfloat16),
                pltpu.VMEM(mine.shape, jnp.bfloat16),
                pltpu.VMEM((2, 4) + pieces[0].shape, jnp.bfloat16),
                pltpu.VMEM((8, groups, size, width), jnp.bfloat16),
                pltpu.SemaphoreType.DMA((2,)),
                pltpu.SemaphoreType.DMA((2, 5)),
                pltpu.SemaphoreType.DMA,
            ],
        ),
        out_shape=jax.ShapeDtypeStruct((groups, 8, size, width), jnp.bfloat16),
        name="panel",
    )(place, mine, other, *pieces)


def shift(value, axis, step):
    count = lax.axis_size(axis)
    return lax.ppermute(value, axis, [(i, (i + step) % count) for i in range(count)])


def trial_pieces(trial):
    z = lax.axis_index("z")
    core = lax.axis_index("core")
    rows, wide = trial.shape
    width = wide // 8
    piece = lax.dynamic_slice_in_dim(trial, (z * 2 + core) * width, width, axis=1)
    piece = piece.reshape(2, 8, rows // 16, width)
    piece = jnp.where(core == 0, piece, piece[::-1])
    piece = jnp.transpose(piece, (1, 0, 2, 3))
    own = lax.all_to_all(piece, COL, split_axis=0, concat_axis=0, tiled=True)
    before = shift(own, "z", 1)
    after = shift(own, "z", -1)
    top = shift(before[:4], "z", 1)
    bottom = shift(after[4:], "z", -1)
    held = (own, before, after, top, bottom)
    return held + tuple(shift(value, "core", 1) for value in held)


def shards(coarse_kernel, interp_index, interp_weight, left_rot, right_rot, trial):
    dev_count = lax.axis_size(ALL)
    core = lax.axis_index("core").astype(jnp.int32)
    coarse_per = coarse_kernel.shape[0]
    pieces = trial_pieces(trial)
    ref_ids = interp_index.reshape(-1)
    catalog = jnp.arange(dev_count * coarse_per, dtype=jnp.int32)
    needed = (
        jnp.any(ref_ids[:, None] == catalog[None, :], axis=0)
        .astype(jnp.int32)
        .reshape(dev_count, coarse_per)
    )
    slot_rank = jnp.cumsum(needed, axis=1) - needed
    picker = needed[:, :, None] * (
        slot_rank[:, :, None] == jnp.arange(CAP, dtype=jnp.int32)[None, None, :]
    ).astype(jnp.int32)
    wanted = jnp.sum(picker * jnp.arange(coarse_per, dtype=jnp.int32)[None, :, None], axis=1)
    requested = lax.all_to_all(wanted, ALL, split_axis=0, concat_axis=0, tiled=True)
    served = serve(requested.reshape(-1), coarse_kernel).reshape(
        (dev_count, CAP) + coarse_kernel.shape[1:]
    )
    arrived = lax.all_to_all(served, ALL, split_axis=0, concat_axis=0, tiled=True)
    arrived = arrived.reshape((dev_count * CAP,) + coarse_kernel.shape[1:])
    slot_table = (jnp.arange(dev_count, dtype=jnp.int32)[:, None] * CAP + slot_rank).reshape(-1)
    ref_slots = jnp.take(slot_table, ref_ids, mode="clip")
    mine, theirs = rotate(
        core.reshape(1), ref_slots, interp_weight.reshape(-1), arrived, left_rot, right_rot
    )
    other = shift(theirs, "core", 1)
    place = jnp.stack([lax.axis_index("z").astype(jnp.int32), core])
    partial_product = panel_product(place, mine, other, pieces)
    groups, parts, size, width = partial_product.shape
    shares = lax.all_to_all(
        partial_product.reshape(groups * parts, size, width),
        SAME_CORE, split_axis=0, concat_axis=0, tiled=True,
    )
    shares = shares.reshape(groups, parts, size, width).astype(jnp.float32)
    return jnp.sum(shares, axis=1).reshape(groups * size, width)


def solution(mesh):
    cube = Mesh(mesh.devices.reshape(2, 4, 2, 4, 2), ALL)
    rows, cols = ALL[:3], ALL[3:]
    return jax.shard_map(
        shards,
        mesh=cube,
        in_specs=(
            P(ALL, None, None),
            P(ALL, None),
            P(ALL, None),
            P(ALL, None, None),
            P(ALL, None, None),
            P(cols, None),
        ),
        out_specs=P(rows, cols),
        check_vma=False,
    )
```

time: 296 us -> 271 us (0.916)
  blocking collectives: 139 us -> 61.4 us
  waiting for transfers between devices: 102 us -> 126 us
  starting transfers between devices: 5.94 us -> 29.3 us
  local copies, waits for them, and re-layouts: 7.79 us -> 12.9 us
    all_to_all x3 -> x1, blocking collectives: 139 us -> 61.4 us  [shards(): lax.all_to_all(partial_product.reshape(groups * parts, size, width), SAME...]
    all_to_all x1 -> x3, starting transfers between devices: 5.94 us -> 21.2 us  [the longest x1 11.2 us: shards(): lax.all_to_all(wanted, ALL, split_axis=0, concat_axis=0, tiled=True)]
    ppermute x0 -> x10, waiting for transfers between devices: none -> 12.4 us  [shift(): lax.ppermute(value, axis, [(i, (i + step) % count) for i in range(count)])]
    all_to_all x1 -> x3, waiting for transfers between devices: 102 us -> 114 us  [the longest x1 98.3 us: shards(): lax.all_to_all(served, ALL, split_axis=0, concat_axis=0, tiled=True)]
    ppermute x0 -> x10, starting transfers between devices: none -> 8.14 us  [shift(): lax.ppermute(value, axis, [(i, (i + step) % count) for i in range(count)])]
    pallas_call x1, Pallas kernels: 18.3 us -> 14.1 us  [rotate(): pl.pallas_call(rotate_kernel, grid_spec=pltpu.PrefetchScalarGridSpec(num_...]
    unnamed x4 -> x22, local copies, waits for them, and re-layouts: 0.91 us -> 3.9 us
  transfers between devices with their start and end apart: 1 -> 13, of which waited for: 1 -> 5; matrix products, arithmetic and copies ran while one was open for 2% -> 4% of each run, Pallas kernels for 0% -> 7%
where the time goes in v2:
time: 271 us; the launch traced here: 270 us
  waiting for transfers between devices  126 us (46%)
  blocking collectives  61.4 us (23%)
  Pallas kernels  35.1 us (13%)
  starting transfers between devices  29.3 us (11%)
  local copies, waits for them, and re-layouts  12.9 us (5%)
  other arithmetic  5.22 us (2%)
    all_to_all x1, waiting for transfers between devices, shards(): lax.all_to_all(served, ALL, split_axis=0, concat_axis=0, tiled=True)  98.3 us
    all_to_all x1, blocking collectives, shards(): lax.all_to_all(partial_product.reshape(groups * parts, size, width), SAME...  61.4 us
    pallas_call x1, Pallas kernels, panel_product(): pl.pallas_call(panel_kernel, grid_spec=pltpu.PrefetchScalarGridSpec(num_s...  16 us
    pallas_call x1, Pallas kernels, rotate(): pl.pallas_call(rotate_kernel, grid_spec=pltpu.PrefetchScalarGridSpec(num_...  14.1 us
    ppermute x10, waiting for transfers between devices, shift(): lax.ppermute(value, axis, [(i, (i + step) % count) for i in range(count)])  12.4 us
    all_to_all x1, starting transfers between devices, shards(): lax.all_to_all(wanted, ALL, split_axis=0, concat_axis=0, tiled=True)  11.2 us
    all_to_all x1, waiting for transfers between devices, trial_pieces(): own = lax.all_to_all(piece, COL, split_axis=0, concat_axis=0, tiled=True)  8.65 us
    ppermute x10, starting transfers between devices, shift(): lax.ppermute(value, axis, [(i, (i + step) % count) for i in range(count)])  8.14 us
  transfers between devices with their start and end apart: 13, of which 5 were waited for; matrix products, arithmetic and copies ran while one was open for 4% of the time, Pallas kernels for 7%

profile of v2, /device:TPU:0, one launch (start us, length us, event | category | flops | bytes accessed | tf_op | source)
XLA Modules:
  0.0 270.3 jit_solution(10256611666795647039)
XLA Ops:
  0.0 0.8 copy.25
  1.9 0.8 copy.31
  2.6 11.2 %all-to-all-start = ((s32[128,1,2]{2,1,0:T(1,128)}), s32[128,1,2]{2,1,0:T(1,128)S(1)}, u32[]{:S(2)}, u32[]{:S(2)}) async-start(s32[128,1,2]{2,1,0:T(1,128)} %copy.31), calls=%async_computation | async-start | bytes 131072 | tf_op jit(solution)/shard_map/all_to_all | solution.py:259
  13.8 1.3 constant_dynamic-slice_fusion
  15.2 1.2 fusion.1
  16.4 6.8 %all-to-all-done = s32[128,1,2]{2,1,0:T(1,128)S(1)} async-done(((s32[128,1,2]{2,1,0:T(1,128)}), s32[128,1,2]{2,1,0:T(1,128)S(1)}, u32[]{:S(2)}, u32[]{:S(2)}) %all-to-all-start) | async-done | bytes 1056 | tf_op jit(solution)/shard_map/all_to_all | solution.py:259
  23.2 3.6 %all-to-all-start.2 = ((bf16[8,2,128,256]{3,2,1,0:T(8,128)(2,1)}), bf16[8,2,128,256]{3,2,1,0:T(8,128)(2,1)S(1)}, u32[]{:S(2)}, u32[]{:S(2)}) async-start(bf16[8,2,128,256]{3,2,1,0:T(8,128)(2,1)} %fusion.1), calls=%async_computation.2 | async-start | bytes 2097152 | tf_op jit(solution)/shard_map/all_to_all | solution.py:233
  27.3 0.8 reduce.3
  28.8 5.0 %serve.1 = bf16[256,128,128]{2,1,0:T(8,128)(2,1)} custom-call(s32[256]{0:T(256)} %reshape.55.wanted, bf16[16,128,128]{2,1,0:T(8,128)(2,1)} %coarse.1), custom_call_target="tpu_custom_call" | custom-call | tf_op jit(solution)/shard_map/serve/pallas_call | solution.py:29
  33.8 8.7 %all-to-all-done.2.refs_0_ = bf16[8,2,128,256]{3,2,1,0:T(8,128)(2,1)S(1)} async-done(((bf16[8,2,128,256]{3,2,1,0:T(8,128)(2,1)}), bf16[8,2,128,256]{3,2,1,0:T(8,128)(2,1)S(1)}, u32[]{:S(2)}, u32[]{:S(2)}) %all-to-all-start.2) | async-done | bytes 1048608 | tf_op jit(solution)/shard_map/all_to_all | solution.py:233
  42.4 6.4 %all-to-all-start.1 = ((bf16[128,2,128,128]{3,2,1,0:T(8,128)(2,1)}), bf16[128,2,128,128]{3,2,1,0:T(8,128)(2,1)}, u32[]{:S(2)}, u32[]{:S(2)}) async-start(bf16[128,2,128,128]{3,2,1,0:T(8,128)(2,1)} %bitcast.13), calls=%async_computation.1 | async-start | bytes 16777216 | tf_op jit(solution)/shard_map/all_to_all | solution.py:263
  50.1 4.3 %gather_fusion = s32[512]{0:T(512)} fusion(s32[2048]{0:T(1024)S(1)} %subtract_add_fusion, s32[1024]{0:T(1024)S(1)} %pad_clamp_fusion), kind=kCustom, calls=%fused_computation | custom fusion | bytes 6144 | tf_op jit(solution)/shard_map/jit(_take)/gather | solution.py:266
  54.4 1.0 collective-permute-start.1
  55.4 2.2 collective-permute-start.2
  57.6 98.3 %all-to-all-done.1 = bf16[128,2,128,128]{3,2,1,0:T(8,128)(2,1)} async-done(((bf16[128,2,128,128]{3,2,1,0:T(8,128)(2,1)}), bf16[128,2,128,128]{3,2,1,0:T(8,128)(2,1)}, u32[]{:S(2)}, u32[]{:S(2)}) %all-to-all-start.1) | async-done | bytes 8388640 | tf_op jit(solution)/shard_map/all_to_all | solution.py:263
  156.0 14.1 %rotate.1 = (bf16[64,128,128]{2,1,0:T(8,128)(2,1)}, bf16[64,128,128]{2,1,0:T(8,128)(2,1)}) custom-call(s32[1]{0:T(128)} %bitcast.1.core, s32[512]{0:T(512)} %gather_fusion, f32[512]{0:T(512)} %reshape.54.weights, bf16[256,128,128]{2,1,0:T(8,128)(2,1)} %bitcast.4.arrived, bf16[128,128,128]{2,1,0:T(8,128)(2,1)} %left.1, bf16[128,128,128]{2,1,0:T(8,128)(2,1)} %right.1), custom_call_target="tpu_custom_call" | custom-call | tf_op jit(solution)/shard_map/rotate/pallas_call | solution.py:114
  171.0 4.1 %collective-permute-start.4 = (bf16[4,2,128,256]{3,2,1,0:T(8,128)(2,1)S(1)}, bf16[4,2,128,256]{3,2,1,0:T(8,128)(2,1)S(1)}, u32[]{:S(2)}, u32[]{:S(2)}) collective-permute-start(bf16[4,2,128,256]{3,2,1,0:T(8,128)(2,1)S(1)} %slice.11), channel_id=1, source_target_pairs={{0,48},{16,0},{32,16},{48,32},{1,49},{17,1},{33,17},{49,33},{2,50}... | collective-permute-start | bytes 1572872 | tf_op jit(solution)/shard_map/ppermute | solution.py:221
  175.1 11.8 %collective-permute-done.3.refs_3_ = bf16[4,2,128,256]{3,2,1,0:T(8,128)(2,1)S(1)} collective-permute-done((bf16[4,2,128,256]{3,2,1,0:T(8,128)(2,1)S(1)}, bf16[4,2,128,256]{3,2,1,0:T(8,128)(2,1)S(1)}, u32[]{:S(2)}, u32[]{:S(2)}) %collective-permute-start.3) | collective-permute-done | bytes 524320 | tf_op jit(solution)/shard_map/ppermute | solution.py:221
  188.1 1.1 copy-done.3
  189.2 1.0 copy-done.4
  190.2 0.8 copy-done.8
  191.1 16.0 %panel.1 = bf16[8,8,128,256]{3,2,1,0:T(8,128)(2,1)} custom-call(s32[2]{0:T(128)} %pad_add_fusion.place, bf16[64,128,128]{2,1,0:T(8,128)(2,1)} %get-tuple-element.7.mine, bf16[64,128,128]{2,1,0:T(8,128)(2,1)} %collective-permute-done.other, bf16[8,2,128,256]{3,2,1,0:T(8,128)(2,1)} %copy-done, bf16[8,2,128,256]{3,2,1,0:T(8,128)(2,1)} %copy-done.1, ...), custom_call_target="tpu_custom_call" | custom-call | tf_op jit(solution)/shard_map/panel/pallas_call | solution.py:197
  207.1 61.4 %all_to_all.24 = bf16[64,128,256]{2,1,0:T(8,128)(2,1)S(1)} all-to-all(bf16[64,128,256]{2,1,0:T(8,128)(2,1)} %bitcast.14), channel_id=1, replica_groups=mesh['ylo'=2,'z'=4,'core'=2,'x'=4,'yhi'=2] {'ylo','z','x','yhi'}, dimensions={0} | all-to-all | bytes 8388608 | tf_op jit(solution)/shard_map/all_to_all | solution.py:274
  268.6 1.7 convert_reduce_fusion
  (56 shorter events, 5.8 us)
Async XLA Ops:
  2.6 20.6 %all-to-all-start = ((s32[128,1,2]{2,1,0:T(1,128)}), s32[128,1,2]{2,1,0:T(1,128)S(1)}, u32[]{:S(2)}, u32[]{:S(2)}) async-start(s32[128,1,2]{2,1,0:T(1,128)} %copy.31), calls=%async_computation | async-start | bytes 131072 | tf_op jit(solution)/shard_map/all_to_all | solution.py:259
  23.2 19.2 %all-to-all-start.2 = ((bf16[8,2,128,256]{3,2,1,0:T(8,128)(2,1)}), bf16[8,2,128,256]{3,2,1,0:T(8,128)(2,1)S(1)}, u32[]{:S(2)}, u32[]{:S(2)}) async-start(bf16[8,2,128,256]{3,2,1,0:T(8,128)(2,1)} %fusion.1), calls=%async_computation.2 | async-start | bytes 2097152 | tf_op jit(solution)/shard_map/all_to_all | solution.py:233
  42.4 15.2 %copy-start = (bf16[8,2,128,256]{3,2,1,0:T(8,128)(2,1)}, bf16[8,2,128,256]{3,2,1,0:T(8,128)(2,1)S(1)}, u32[]{:S(2)}) copy-start(bf16[8,2,128,256]{3,2,1,0:T(8,128)(2,1)S(1)} %all-to-all-done.2.refs_0_) | copy-start | bytes 3145732
  42.4 6.8 %copy-start.9 = (f32[128,4]{0,1:T(4,128)S(1)}, f32[128,4]{0,1:T(4,128)}, u32[]{:S(2)}) copy-start(f32[128,4]{0,1:T(4,128)} %param.8) | copy-start | bytes 6148
  42.4 113.5 %all-to-all-start.1 = ((bf16[128,2,128,128]{3,2,1,0:T(8,128)(2,1)}), bf16[128,2,128,128]{3,2,1,0:T(8,128)(2,1)}, u32[]{:S(2)}, u32[]{:S(2)}) async-start(bf16[128,2,128,128]{3,2,1,0:T(8,128)(2,1)} %bitcast.13), calls=%async_computation.1 | async-start | bytes 16777216 | tf_op jit(solution)/shard_map/all_to_all | solution.py:263
  54.4 115.8 %collective-permute-start.1 = (bf16[8,2,128,256]{3,2,1,0:T(8,128)(2,1)S(1)}, bf16[8,2,128,256]{3,2,1,0:T(8,128)(2,1)S(1)}, u32[]{:S(2)}, u32[]{:S(2)}) collective-permute-start(bf16[8,2,128,256]{3,2,1,0:T(8,128)(2,1)S(1)} %all-to-all-done.2.refs_0_), channel_id=1, source_target_pairs={{0,16},{16,32},{32,48},{48,0},{1,17},{17,33},{33,49},{49,1},{2,18}... | collective-permute-start | bytes 3145736 | tf_op jit(solution)/shard_map/ppermute | solution.py:221
  55.4 115.5 %collective-permute-start.2 = (bf16[8,2,128,256]{3,2,1,0:T(8,128)(2,1)S(1)}, bf16[8,2,128,256]{3,2,1,0:T(8,128)(2,1)S(1)}, u32[]{:S(2)}, u32[]{:S(2)}) collective-permute-start(bf16[8,2,128,256]{3,2,1,0:T(8,128)(2,1)S(1)} %all-to-all-done.2.refs_0_), channel_id=1, source_target_pairs={{0,48},{16,0},{32,16},{48,32},{1,49},{17,1},{33,17},{49,33},{2,50}... | collective-permute-start | bytes 3145736 | tf_op jit(solution)/shard_map/ppermute | solution.py:221
  57.6 113.4 %collective-permute-start.5 = (bf16[8,2,128,256]{3,2,1,0:T(8,128)(2,1)S(1)}, bf16[8,2,128,256]{3,2,1,0:T(8,128)(2,1)}, u32[]{:S(2)}, u32[]{:S(2)}) collective-permute-start(bf16[8,2,128,256]{3,2,1,0:T(8,128)(2,1)S(1)} %all-to-all-done.2.refs_0_), channel_id=1, source_target_pairs={{0,8},{8,0},{1,9},{9,1},{2,10},{10,2},{3,11},{11,3},{4,12},{12,4},... | collective-permute-start | bytes 3145736 | tf_op jit(solution)/shard_map/ppermute | solution.py:221
  170.1 20.1 %collective-permute-start = (bf16[64,128,128]{2,1,0:T(8,128)(2,1)}, bf16[64,128,128]{2,1,0:T(8,128)(2,1)}, u32[]{:S(2)}, u32[]{:S(2)}) collective-permute-start(bf16[64,128,128]{2,1,0:T(8,128)(2,1)} %get-tuple-element.8), channel_id=1, source_target_pairs={{0,8},{8,0},{1,9},{9,1},{2,10},{10,2},{3,11},{11,3},{4,12},{12,4},... | collective-permute-start | bytes 6291464 | tf_op jit(solution)/shard_map/ppermute | solution.py:221
  170.2 20.8 %copy-start.1 = (bf16[8,2,128,256]{3,2,1,0:T(8,128)(2,1)}, bf16[8,2,128,256]{3,2,1,0:T(8,128)(2,1)S(1)}, u32[]{:S(2)}) copy-start(bf16[8,2,128,256]{3,2,1,0:T(8,128)(2,1)S(1)} %collective-permute-done.1.refs_1_) | copy-start | bytes 3145732
  170.2 16.6 %collective-permute-start.3 = (bf16[4,2,128,256]{3,2,1,0:T(8,128)(2,1)S(1)}, bf16[4,2,128,256]{3,2,1,0:T(8,128)(2,1)S(1)}, u32[]{:S(2)}, u32[]{:S(2)}) collective-permute-start(bf16[4,2,128,256]{3,2,1,0:T(8,128)(2,1)S(1)} %slice.10), channel_id=1, source_target_pairs={{0,16},{16,32},{32,48},{48,0},{1,17},{17,33},{33,49},{49,1},{2,18}... | collective-permute-start | bytes 1572872 | tf_op jit(solution)/shard_map/ppermute | solution.py:221
  170.3 17.8 %collective-permute-start.6 = (bf16[8,2,128,256]{3,2,1,0:T(8,128)(2,1)S(1)}, bf16[8,2,128,256]{3,2,1,0:T(8,128)(2,1)S(1)}, u32[]{:S(2)}, u32[]{:S(2)}) collective-permute-start(bf16[8,2,128,256]{3,2,1,0:T(8,128)(2,1)S(1)} %collective-permute-done.1.refs_1_), channel_id=1, source_target_pairs={{0,8},{8,0},{1,9},{9,1},{2,10},{10,2},{3,11},{11,3},{4,12},{12,4},... | collective-permute-start | bytes 3145736 | tf_op jit(solution)/shard_map/ppermute | solution.py:221
  170.9 20.1 %copy-start.2 = (bf16[8,2,128,256]{3,2,1,0:T(8,128)(2,1)}, bf16[8,2,128,256]{3,2,1,0:T(8,128)(2,1)S(1)}, u32[]{:S(2)}) copy-start(bf16[8,2,128,256]{3,2,1,0:T(8,128)(2,1)S(1)} %collective-permute-done.2.refs_2_) | copy-start | bytes 3145732
  170.9 17.2 %collective-permute-start.7 = (bf16[8,2,128,256]{3,2,1,0:T(8,128)(2,1)S(1)}, bf16[8,2,128,256]{3,2,1,0:T(8,128)(2,1)S(1)}, u32[]{:S(2)}, u32[]{:S(2)}) collective-permute-start(bf16[8,2,128,256]{3,2,1,0:T(8,128)(2,1)S(1)} %collective-permute-done.2.refs_2_), channel_id=1, source_target_pairs={{0,8},{8,0},{1,9},{9,1},{2,10},{10,2},{3,11},{11,3},{4,12},{12,4},... | collective-permute-start | bytes 3145736 | tf_op jit(solution)/shard_map/ppermute | solution.py:221
  171.0 16.4 %collective-permute-start.4 = (bf16[4,2,128,256]{3,2,1,0:T(8,128)(2,1)S(1)}, bf16[4,2,128,256]{3,2,1,0:T(8,128)(2,1)S(1)}, u32[]{:S(2)}, u32[]{:S(2)}) collective-permute-start(bf16[4,2,128,256]{3,2,1,0:T(8,128)(2,1)S(1)} %slice.11), channel_id=1, source_target_pairs={{0,48},{16,0},{32,16},{48,32},{1,49},{17,1},{33,17},{49,33},{2,50}... | collective-permute-start | bytes 1572872 | tf_op jit(solution)/shard_map/ppermute | solution.py:221
  186.9 3.3 %copy-start.5 = (bf16[4,2,128,256]{3,2,1,0:T(8,128)(2,1)}, bf16[4,2,128,256]{3,2,1,0:T(8,128)(2,1)S(1)}, u32[]{:S(2)}) copy-start(bf16[4,2,128,256]{3,2,1,0:T(8,128)(2,1)S(1)} %collective-permute-done.3.refs_3_) | copy-start | bytes 1572868
  186.9 2.3 collective-permute-start.8
  187.4 3.6 %copy-start.6 = (bf16[4,2,128,256]{3,2,1,0:T(8,128)(2,1)}, bf16[4,2,128,256]{3,2,1,0:T(8,128)(2,1)S(1)}, u32[]{:S(2)}) copy-start(bf16[4,2,128,256]{3,2,1,0:T(8,128)(2,1)S(1)} %collective-permute-done.4.refs_4_) | copy-start | bytes 1572868
  187.4 2.7 %collective-permute-start.9 = (bf16[4,2,128,256]{3,2,1,0:T(8,128)(2,1)S(1)}, bf16[4,2,128,256]{3,2,1,0:T(8,128)(2,1)S(1)}, u32[]{:S(2)}, u32[]{:S(2)}) collective-permute-start(bf16[4,2,128,256]{3,2,1,0:T(8,128)(2,1)S(1)} %collective-permute-done.4.refs_4_), channel_id=1, source_target_pairs={{0,8},{8,0},{1,9},{9,1},{2,10},{10,2},{3,11},{11,3},{4,12},{12,4},... | collective-permute-start | bytes 1572872 | tf_op jit(solution)/shard_map/ppermute | solution.py:221
  188.1 1.1 copy-start.3
  189.2 1.0 copy-start.4
  190.2 1.0 copy-start.7
  190.2 0.8 copy-start.8

commit v3 on v2

v3 whole, which is shorter than its diff:
```python
import jax
import jax.numpy as jnp
from jax import lax
from jax.experimental import pallas as pl
from jax.experimental.pallas import tpu as pltpu
from jax.sharding import Mesh, PartitionSpec as P

CAP = 2
CHUNKS = 4
ROOM = 24 * 2**20
ALL = ("ylo", "z", "core", "x", "yhi")
COL = ("x", "yhi")
SAME_CORE = ("ylo", "z", "x", "yhi")


def serve_kernel(wanted, coarse, out, sem):
    def issue(i, carry):
        pltpu.make_async_copy(coarse.at[wanted[i]], out.at[i], sem).start()
        return carry

    lax.fori_loop(0, out.shape[0], issue, 0, unroll=8)
    pltpu.make_async_copy(out, out, sem).wait()


def serve(wanted, coarse_kernel):
    count = wanted.shape[0]
    return pl.pallas_call(
        serve_kernel,
        grid_spec=pltpu.PrefetchScalarGridSpec(
            num_scalar_prefetch=1,
            grid=(),
            in_specs=[pl.BlockSpec(memory_space=pltpu.VMEM)],
            out_specs=pl.BlockSpec(memory_space=pl.ANY),
            scratch_shapes=[pltpu.SemaphoreType.DMA],
        ),
        out_shape=pltpu.HBM((count,) + coarse_kernel.shape[1:], coarse_kernel.dtype),
        name="serve",
    )(wanted, coarse_kernel)


def near(value):
    return pltpu.with_memory_space_constraint(value, pltpu.VMEM)


def far(value):
    return pltpu.with_memory_space_constraint(value, pltpu.HBM)


def split(value):
    high = value.astype(jnp.bfloat16)
    low = (value - high.astype(jnp.float32)).astype(jnp.bfloat16)
    return high, low


def rotate_kernel(
    core, slots, weights, arrived, left, right, mine, theirs, left_v, right_v, sem_left, sem_right
):
    blocks = left.shape[0]
    span = blocks // CHUNKS
    copies = []
    for n in range(CHUNKS):
        part = pl.ds(n * span, span)
        pair = (
            pltpu.make_async_copy(left.at[part], left_v.at[part], sem_left.at[n]),
            pltpu.make_async_copy(right.at[part], right_v.at[part], sem_right.at[n]),
        )
        for copy in pair:
            copy.start()
        copies.append(pair)

    def block(f, out, place):
        r = f * 4
        merged = weights[r] * arrived[slots[r]].astype(jnp.float32)
        for j in range(1, 4):
            merged += weights[r + j] * arrived[slots[r + j]].astype(jnp.float32)
        lhs = left_v[f]
        turned = jnp.dot(
            jnp.concatenate([lhs, lhs], axis=1),
            jnp.concatenate(split(merged), axis=0),
            preferred_element_type=jnp.float32,
        )
        rhs = right_v[f]
        fine = lax.dot_general(
            jnp.concatenate(split(turned), axis=1),
            jnp.concatenate([rhs, rhs], axis=1),
            (((1,), (1,)), ((), ())),
            preferred_element_type=jnp.float32,
        )
        out[place] = fine.astype(jnp.bfloat16)

    for n in range(CHUNKS):
        for copy in copies[n]:
            copy.wait()

        def several(i, carry):
            group = n * (span // 16) + i
            for k in range(8):
                block(group * 16 + core[0] * 8 + k, mine, group * 8 + k)
                block(group * 16 + (1 - core[0]) * 8 + k, theirs, group * 8 + k)
            return carry

        lax.fori_loop(0, span // 16, several, 0)


def rotate(core, slots, weights, arrived, left, right):
    half = jax.ShapeDtypeStruct((left.shape[0] // 2,) + left.shape[1:], jnp.bfloat16)
    anywhere = pl.BlockSpec(memory_space=pl.ANY)
    local = pl.BlockSpec(memory_space=pltpu.VMEM)
    return pl.pallas_call(
        rotate_kernel,
        grid_spec=pltpu.PrefetchScalarGridSpec(
            num_scalar_prefetch=3,
            grid=(),
            in_specs=[local, anywhere, anywhere],
            out_specs=[local, local],
            scratch_shapes=[
                pltpu.VMEM(left.shape, jnp.bfloat16),
                pltpu.VMEM(left.shape, jnp.bfloat16),
                pltpu.SemaphoreType.DMA((CHUNKS,)),
                pltpu.SemaphoreType.DMA((CHUNKS,)),
            ],
        ),
        out_shape=[half, half],
        compiler_params=pltpu.CompilerParams(vmem_limit_bytes=ROOM),
        name="rotate",
    )(core, slots, weights, arrived, far(left), far(right))


def panel_kernel(place, mine, other, *refs):
    pieces, out, out_v, sem = refs[:14], refs[14], refs[15], refs[16]
    groups = mine.shape[0] // 8
    for side in range(2):
        held = pieces[side * 7 : side * 7 + 7]
        own, before, after, beyond = held[:1], held[1:3], held[3:5], held[5:]
        order = (mine, other) if side == 0 else (other, mine)
        core = place[1] if side == 0 else 1 - place[1]
        for rel, parts in enumerate((own, after, beyond, before)):
            lhs = jnp.concatenate(
                [
                    jnp.concatenate(
                        [
                            order[q][g * 8 + n]
                            for n in range(8)
                            for q in range(2)
                        ],
                        axis=1,
                    )
                    for g in range(groups)
                ],
                axis=0,
            )
            rhs = jnp.concatenate([p[...].reshape(-1, p.shape[-1]) for p in parts], axis=0)
            slot = side * 4 + rel
            out_v[slot] = (
                jnp.dot(lhs, rhs, preferred_element_type=jnp.float32)
                .astype(jnp.bfloat16)
                .reshape(out_v.shape[1:])
            )
            target = lax.rem(place[0] + rel, 4) * 2 + core
            pltpu.make_async_copy(out_v.at[slot], out.at[:, target], sem).start()
    pltpu.make_async_copy(out_v, out_v, sem).wait()


def panel_product(place, mine, other, pieces):
    groups = mine.shape[0] // 8
    size = mine.shape[1]
    width = pieces[0].shape[-1]
    local = pl.BlockSpec(memory_space=pltpu.VMEM)
    return pl.pallas_call(
        panel_kernel,
        grid_spec=pltpu.PrefetchScalarGridSpec(
            num_scalar_prefetch=1,
            grid=(),
            in_specs=[local] * (2 + len(pieces)),
            out_specs=pl.BlockSpec(memory_space=pl.ANY),
            scratch_shapes=[
                pltpu.VMEM((8, groups, size, width), jnp.bfloat16),
                pltpu.SemaphoreType.DMA,
            ],
        ),
        out_shape=pltpu.HBM((groups, 8, size, width), jnp.bfloat16),
        compiler_params=pltpu.CompilerParams(vmem_limit_bytes=ROOM),
        name="panel",
    )(place, mine, near(other), *map(near, pieces))


def shift(value, axis, step):
    count = lax.axis_size(axis)
    return lax.ppermute(value, axis, [(i, (i + step) % count) for i in range(count)])


def trial_pieces(trial):
    z = lax.axis_index("z")
    core = lax.axis_index("core")
    rows, wide = trial.shape
    width = wide // 8
    piece = lax.dynamic_slice_in_dim(trial, (z * 2 + core) * width, width, axis=1)
    piece = piece.reshape(2, 8, rows // 16, width)
    piece = jnp.where(core == 0, piece, piece[::-1])
    piece = jnp.transpose(piece, (1, 0, 2, 3))
    own = lax.all_to_all(piece, COL, split_axis=0, concat_axis=0, tiled=True)
    halves = own[:4], own[4:]
    before = [shift(half, "z", 1) for half in halves]
    after = [shift(half, "z", -1) for half in halves]
    top = shift(before[0], "z", 1)
    bottom = shift(after[1], "z", -1)
    early = [shift(value, "core", 1) for value in (own, *before, *after)]
    late = [shift(value, "core", 1) for value in (top, bottom)]
    return (own, *before, *after, top, bottom, *early, *late)


def shards(coarse_kernel, interp_index, interp_weight, left_rot, right_rot, trial):
    dev_count = lax.axis_size(ALL)
    core = lax.axis_index("core").astype(jnp.int32)
    coarse_per = coarse_kernel.shape[0]
    place = jnp.stack([lax.axis_index("z").astype(jnp.int32), core])
    pieces = trial_pieces(trial)
    ref_ids = interp_index.reshape(-1)
    catalog = jnp.arange(dev_count * coarse_per, dtype=jnp.int32)
    needed = (
        jnp.any(ref_ids[:, None] == catalog[None, :], axis=0)
        .astype(jnp.int32)
        .reshape(dev_count, coarse_per)
    )
    slot_rank = jnp.cumsum(needed, axis=1) - needed
    picker = needed[:, :, None] * (
        slot_rank[:, :, None] == jnp.arange(CAP, dtype=jnp.int32)[None, None, :]
    ).astype(jnp.int32)
    wanted = jnp.sum(picker * jnp.arange(coarse_per, dtype=jnp.int32)[None, :, None], axis=1)
    requested = lax.all_to_all(wanted, ALL, split_axis=0, concat_axis=0, tiled=True)
    served = serve(requested.reshape(-1), coarse_kernel).reshape(
        (dev_count, CAP) + coarse_kernel.shape[1:]
    )
    arrived = lax.all_to_all(served, ALL, split_axis=0, concat_axis=0, tiled=True)
    arrived = arrived.reshape((dev_count * CAP,) + coarse_kernel.shape[1:])
    slot_table = (jnp.arange(dev_count, dtype=jnp.int32)[:, None] * CAP + slot_rank).reshape(-1)
    ref_slots = jnp.take(slot_table, ref_ids, mode="clip")
    mine, theirs = rotate(
        core.reshape(1), ref_slots, interp_weight.reshape(-1), arrived, left_rot, right_rot
    )
    other = shift(theirs, "core", 1)
    partial_product = panel_product(place, mine, other, pieces)
    groups, parts, size, width = partial_product.shape
    shares = lax.all_to_all(
        partial_product.reshape(groups * parts, size, width),
        SAME_CORE, split_axis=0, concat_axis=0, tiled=True,
    )
    shares = shares.reshape(groups, parts, size, width).astype(jnp.float32)
    return jnp.sum(shares, axis=1).reshape(groups * size, width)


def solution(mesh):
    cube = Mesh(mesh.devices.reshape(2, 4, 2, 4, 2), ALL)
    rows, cols = ALL[:3], ALL[3:]
    return jax.shard_map(
        shards,
        mesh=cube,
        in_specs=(
            P(ALL, None, None),
            P(ALL, None),
            P(ALL, None),
            P(ALL, None, None),
            P(ALL, None, None),
            P(cols, None),
        ),
        out_specs=P(rows, cols),
        check_vma=False,
    )
```

time: 271 us -> 286 us (1.055)
  waiting for transfers between devices: 126 us -> 147 us
  Pallas kernels: 35.1 us -> 28.1 us
  starting transfers between devices: 29.3 us -> 35.6 us
  local copies, waits for them, and re-layouts: 12.9 us -> 8.22 us
    ppermute x10 -> x14, waiting for transfers between devices: 12.4 us -> 30.9 us  [shift(): lax.ppermute(value, axis, [(i, (i + step) % count) for i in range(count)])]
    ppermute x10 -> x14, starting transfers between devices: 8.14 us -> 14.4 us  [shift(): lax.ppermute(value, axis, [(i, (i + step) % count) for i in range(count)])]
    pallas_call x1, Pallas kernels: 16 us -> 10.5 us  [panel_product(): pl.pallas_call(panel_kernel, grid_spec=pltpu.PrefetchScalarGridSpec(num_s...]
    unnamed x22 -> x4, local copies, waits for them, and re-layouts: 3.9 us -> 0.9 us
  transfers between devices with their start and end apart: 13 -> 17, of which waited for: 5 -> 9; matrix products, arithmetic and copies ran while one was open for 4% -> 3% of each run, Pallas kernels for 7% -> 6%
where the time goes in v3:
time: 286 us; the launch traced here: 285 us
  waiting for transfers between devices  147 us (51%)
  blocking collectives  62 us (22%)
  starting transfers between devices  35.6 us (12%)
  Pallas kernels  28.1 us (10%)
  local copies, waits for them, and re-layouts  8.22 us (3%)
  other arithmetic  4.63 us (2%)
    all_to_all x1, waiting for transfers between devices, shards(): lax.all_to_all(served, ALL, split_axis=0, concat_axis=0, tiled=True)  100 us
    all_to_all x1, blocking collectives, shards(): lax.all_to_all(partial_product.reshape(groups * parts, size, width), SAME...  62 us
    ppermute x14, waiting for transfers between devices, shift(): lax.ppermute(value, axis, [(i, (i + step) % count) for i in range(count)])  30.9 us
    ppermute x14, starting transfers between devices, shift(): lax.ppermute(value, axis, [(i, (i + step) % count) for i in range(count)])  14.4 us
    pallas_call x1, Pallas kernels, rotate(): pl.pallas_call(rotate_kernel, grid_spec=pltpu.PrefetchScalarGridSpec(num_...  12.6 us
    all_to_all x1, starting transfers between devices, shards(): lax.all_to_all(wanted, ALL, split_axis=0, concat_axis=0, tiled=True)  11.2 us
    pallas_call x1, Pallas kernels, panel_product(): pl.pallas_call(panel_kernel, grid_spec=pltpu.PrefetchScalarGridSpec(num_s...  10.5 us
    all_to_all x1, waiting for transfers between devices, trial_pieces(): own = lax.all_to_all(piece, COL, split_axis=0, concat_axis=0, tiled=True)  8.53 us
  transfers between devices with their start and end apart: 17, of which 9 were waited for; matrix products, arithmetic and copies ran while one was open for 3% of the time, Pallas kernels for 6%

profile of v3, /device:TPU:0, one launch (start us, length us, event | category | flops | bytes accessed | tf_op | source)
XLA Modules:
  0.0 285.4 jit_solution(7119189830170169580)
XLA Ops:
  2.6 11.2 %all-to-all-start = ((s32[128,1,2]{2,1,0:T(1,128)}), s32[128,1,2]{2,1,0:T(1,128)S(1)}, u32[]{:S(2)}, u32[]{:S(2)}) async-start(s32[128,1,2]{2,1,0:T(1,128)} %copy.31), calls=%async_computation | async-start | bytes 131072 | tf_op jit(solution)/shard_map/all_to_all | solution.py:230
  13.8 1.3 constant_dynamic-slice_fusion
  15.2 1.2 fusion.1
  16.4 6.8 %all-to-all-done = s32[128,1,2]{2,1,0:T(1,128)S(1)} async-done(((s32[128,1,2]{2,1,0:T(1,128)}), s32[128,1,2]{2,1,0:T(1,128)S(1)}, u32[]{:S(2)}, u32[]{:S(2)}) %all-to-all-start) | async-done | bytes 1056 | tf_op jit(solution)/shard_map/all_to_all | solution.py:230
  23.2 3.6 %all-to-all-start.2 = ((bf16[8,2,128,256]{3,2,1,0:T(8,128)(2,1)}), bf16[8,2,128,256]{3,2,1,0:T(8,128)(2,1)S(1)}, u32[]{:S(2)}, u32[]{:S(2)}) async-start(bf16[8,2,128,256]{3,2,1,0:T(8,128)(2,1)} %fusion.1), calls=%async_computation.2 | async-start | bytes 2097152 | tf_op jit(solution)/shard_map/all_to_all | solution.py:201
  27.4 0.8 reduce.3
  28.9 5.0 %serve.1 = bf16[256,128,128]{2,1,0:T(8,128)(2,1)} custom-call(s32[256]{0:T(256)} %reshape.55.wanted, bf16[16,128,128]{2,1,0:T(8,128)(2,1)} %coarse.1), custom_call_target="tpu_custom_call" | custom-call | tf_op jit(solution)/shard_map/serve/pallas_call | solution.py:27
  33.9 8.5 %all-to-all-done.2.refs_0_ = bf16[8,2,128,256]{3,2,1,0:T(8,128)(2,1)S(1)} async-done(((bf16[8,2,128,256]{3,2,1,0:T(8,128)(2,1)}), bf16[8,2,128,256]{3,2,1,0:T(8,128)(2,1)S(1)}, u32[]{:S(2)}, u32[]{:S(2)}) %all-to-all-start.2) | async-done | bytes 1048608 | tf_op jit(solution)/shard_map/all_to_all | solution.py:201
  42.5 6.5 %all-to-all-start.1 = ((bf16[128,2,128,128]{3,2,1,0:T(8,128)(2,1)}), bf16[128,2,128,128]{3,2,1,0:T(8,128)(2,1)}, u32[]{:S(2)}, u32[]{:S(2)}) async-start(bf16[128,2,128,128]{3,2,1,0:T(8,128)(2,1)} %bitcast.13), calls=%async_computation.1 | async-start | bytes 16777216 | tf_op jit(solution)/shard_map/all_to_all | solution.py:234
  49.5 3.1 %gather_fusion = s32[512]{0:T(512)S(1)} fusion(s32[2048]{0:T(1024)S(1)} %subtract_add_fusion, s32[1024]{0:T(1024)S(1)} %pad_clamp_fusion), kind=kCustom, calls=%fused_computation | custom fusion | bytes 6144 | tf_op jit(solution)/shard_map/jit(_take)/gather | solution.py:237
  52.8 1.1 collective-permute-start.1
  53.8 1.7 collective-permute-start.2
  55.6 100.4 %all-to-all-done.1 = bf16[128,2,128,128]{3,2,1,0:T(8,128)(2,1)} async-done(((bf16[128,2,128,128]{3,2,1,0:T(8,128)(2,1)}), bf16[128,2,128,128]{3,2,1,0:T(8,128)(2,1)}, u32[]{:S(2)}, u32[]{:S(2)}) %all-to-all-start.1) | async-done | bytes 8388640 | tf_op jit(solution)/shard_map/all_to_all | solution.py:234
  156.0 12.6 %rotate.1 = (bf16[64,128,128]{2,1,0:T(8,128)(2,1)S(1)}, bf16[64,128,128]{2,1,0:T(8,128)(2,1)S(1)}) custom-call(s32[1]{0:T(128)} %bitcast.1.core, s32[512]{0:T(512)S(1)} %gather_fusion, f32[512]{0:T(512)S(1)} %reshape.54.weights, bf16[256,128,128]{2,1,0:T(8,128)(2,1)} %bitcast.4.arrived, bf16[128,128,128]{2,1,0:T(8,128)(2,1)} %left.1, ...), custom_call_target="tpu_custom_call" | custom-call | tf_op jit(solution)/shard_map/rotate/pallas_call | solution.py:109
  168.7 4.1 %collective-permute-start.4 = (bf16[4,2,128,256]{3,2,1,0:T(8,128)(2,1)S(1)}, bf16[4,2,128,256]{3,2,1,0:T(8,128)(2,1)S(1)}, u32[]{:S(2)}, u32[]{:S(2)}) collective-permute-start(bf16[4,2,128,256]{3,2,1,0:T(8,128)(2,1)S(1)} %get-tuple-element.9), channel_id=1, source_target_pairs={{0,48},{16,0},{32,16},{48,32},{1,49},{17,1},{33,17},{49,33},{2,50}... | collective-permute-start | bytes 1572872 | tf_op jit(solution)/shard_map/ppermute | solution.py:189
  173.6 1.3 collective-permute-start.5
  174.9 10.1 %collective-permute-done.4.refs_4_ = bf16[4,2,128,256]{3,2,1,0:T(8,128)(2,1)S(1)} collective-permute-done((bf16[4,2,128,256]{3,2,1,0:T(8,128)(2,1)S(1)}, bf16[4,2,128,256]{3,2,1,0:T(8,128)(2,1)S(1)}, u32[]{:S(2)}, u32[]{:S(2)}) %collective-permute-start.4) | collective-permute-done | bytes 524320 | tf_op jit(solution)/shard_map/ppermute | solution.py:189
  185.1 3.7 %collective-permute-start.6 = (bf16[4,2,128,256]{3,2,1,0:T(8,128)(2,1)S(1)}, bf16[4,2,128,256]{3,2,1,0:T(8,128)(2,1)S(1)}, u32[]{:S(2)}, u32[]{:S(2)}) collective-permute-start(bf16[4,2,128,256]{3,2,1,0:T(8,128)(2,1)S(1)} %collective-permute-done.4.refs_4_), channel_id=1, source_target_pairs={{0,48},{16,0},{32,16},{48,32},{1,49},{17,1},{33,17},{49,33},{2,50}... | collective-permute-start | bytes 1572872 | tf_op jit(solution)/shard_map/ppermute | solution.py:189
  188.8 7.5 %collective-permute-done.3.refs_3_ = bf16[4,2,128,256]{3,2,1,0:T(8,128)(2,1)S(1)} collective-permute-done((bf16[4,2,128,256]{3,2,1,0:T(8,128)(2,1)S(1)}, bf16[4,2,128,256]{3,2,1,0:T(8,128)(2,1)S(1)}, u32[]{:S(2)}, u32[]{:S(2)}) %collective-permute-start.3) | collective-permute-done | bytes 524320 | tf_op jit(solution)/shard_map/ppermute | solution.py:189
  196.8 10.2 %collective-permute-done.6.refs_6_ = bf16[4,2,128,256]{3,2,1,0:T(8,128)(2,1)S(1)} collective-permute-done((bf16[4,2,128,256]{3,2,1,0:T(8,128)(2,1)S(1)}, bf16[4,2,128,256]{3,2,1,0:T(8,128)(2,1)S(1)}, u32[]{:S(2)}, u32[]{:S(2)}) %collective-permute-start.6) | collective-permute-done | bytes 524320 | tf_op jit(solution)/shard_map/ppermute | solution.py:189
  208.1 1.6 collective-permute-done.10.refs_10_
  211.2 10.5 %panel.1 = bf16[8,8,128,256]{3,2,1,0:T(8,128)(2,1)} custom-call(s32[2]{0:T(128)S(1)} %pad_add_fusion.place, bf16[64,128,128]{2,1,0:T(8,128)(2,1)S(1)} %get-tuple-element.7.mine, bf16[64,128,128]{2,1,0:T(8,128)(2,1)S(1)} %collective-permute-done.other, bf16[8,2,128,256]{3,2,1,0:T(8,128)(2,1)S(1)} %all-to-all-done.2.refs_0_, ...), custom_call_target="tpu_custom_call" | custom-call | tf_op jit(solution)/shard_map/panel/pallas_call | solution.py:169
  221.7 62.0 %all_to_all.24 = bf16[64,128,256]{2,1,0:T(8,128)(2,1)S(1)} all-to-all(bf16[64,128,256]{2,1,0:T(8,128)(2,1)} %bitcast.14), channel_id=1, replica_groups=mesh['ylo'=2,'z'=4,'core'=2,'x'=4,'yhi'=2] {'ylo','z','x','yhi'}, dimensions={0} | all-to-all | bytes 8388608 | tf_op jit(solution)/shard_map/all_to_all | solution.py:244
  283.8 1.7 convert_reduce_fusion
  (45 shorter events, 8.7 us)
Async XLA Ops:
  2.6 20.6 %all-to-all-start = ((s32[128,1,2]{2,1,0:T(1,128)}), s32[128,1,2]{2,1,0:T(1,128)S(1)}, u32[]{:S(2)}, u32[]{:S(2)}) async-start(s32[128,1,2]{2,1,0:T(1,128)} %copy.31), calls=%async_computation | async-start | bytes 131072 | tf_op jit(solution)/shard_map/all_to_all | solution.py:230
  23.2 19.2 %all-to-all-start.2 = ((bf16[8,2,128,256]{3,2,1,0:T(8,128)(2,1)}), bf16[8,2,128,256]{3,2,1,0:T(8,128)(2,1)S(1)}, u32[]{:S(2)}, u32[]{:S(2)}) async-start(bf16[8,2,128,256]{3,2,1,0:T(8,128)(2,1)} %fusion.1), calls=%async_computation.2 | async-start | bytes 2097152 | tf_op jit(solution)/shard_map/all_to_all | solution.py:201
  42.5 6.8 %copy-start = (f32[128,4]{0,1:T(4,128)S(1)}, f32[128,4]{0,1:T(4,128)}, u32[]{:S(2)}) copy-start(f32[128,4]{0,1:T(4,128)} %param.8) | copy-start | bytes 6148
  42.5 113.5 %all-to-all-start.1 = ((bf16[128,2,128,128]{3,2,1,0:T(8,128)(2,1)}), bf16[128,2,128,128]{3,2,1,0:T(8,128)(2,1)}, u32[]{:S(2)}, u32[]{:S(2)}) async-start(bf16[128,2,128,128]{3,2,1,0:T(8,128)(2,1)} %bitcast.13), calls=%async_computation.1 | async-start | bytes 16777216 | tf_op jit(solution)/shard_map/all_to_all | solution.py:234
  52.8 120.1 %collective-permute-start.1 = (bf16[4,2,128,256]{3,2,1,0:T(8,128)(2,1)S(1)}, bf16[4,2,128,256]{3,2,1,0:T(8,128)(2,1)S(1)}, u32[]{:S(2)}, u32[]{:S(2)}) collective-permute-start(bf16[4,2,128,256]{3,2,1,0:T(8,128)(2,1)S(1)} %get-tuple-element.10), channel_id=1, source_target_pairs={{0,16},{16,32},{32,48},{48,0},{1,17},{17,33},{33,49},{49,1},{2,18}... | collective-permute-start | bytes 1572872 | tf_op jit(solution)/shard_map/ppermute | solution.py:189
  53.8 119.8 %collective-permute-start.2 = (bf16[4,2,128,256]{3,2,1,0:T(8,128)(2,1)S(1)}, bf16[4,2,128,256]{3,2,1,0:T(8,128)(2,1)S(1)}, u32[]{:S(2)}, u32[]{:S(2)}) collective-permute-start(bf16[4,2,128,256]{3,2,1,0:T(8,128)(2,1)S(1)} %get-tuple-element.9), channel_id=1, source_target_pairs={{0,16},{16,32},{32,48},{48,0},{1,17},{17,33},{33,49},{49,1},{2,18}... | collective-permute-start | bytes 1572872 | tf_op jit(solution)/shard_map/ppermute | solution.py:189
  168.6 42.6 %collective-permute-start = (bf16[64,128,128]{2,1,0:T(8,128)(2,1)S(1)}, bf16[64,128,128]{2,1,0:T(8,128)(2,1)S(1)}, u32[]{:S(2)}, u32[]{:S(2)}) collective-permute-start(bf16[64,128,128]{2,1,0:T(8,128)(2,1)S(1)} %get-tuple-element.8), channel_id=1, source_target_pairs={{0,8},{8,0},{1,9},{9,1},{2,10},{10,2},{3,11},{11,3},{4,12},{12,4},... | collective-permute-start | bytes 6291464 | tf_op jit(solution)/shard_map/ppermute | solution.py:189
  168.7 16.4 %collective-permute-start.4 = (bf16[4,2,128,256]{3,2,1,0:T(8,128)(2,1)S(1)}, bf16[4,2,128,256]{3,2,1,0:T(8,128)(2,1)S(1)}, u32[]{:S(2)}, u32[]{:S(2)}) collective-permute-start(bf16[4,2,128,256]{3,2,1,0:T(8,128)(2,1)S(1)} %get-tuple-element.9), channel_id=1, source_target_pairs={{0,48},{16,0},{32,16},{48,32},{1,49},{17,1},{33,17},{49,33},{2,50}... | collective-permute-start | bytes 1572872 | tf_op jit(solution)/shard_map/ppermute | solution.py:189
  172.8 34.3 %collective-permute-start.7 = (bf16[8,2,128,256]{3,2,1,0:T(8,128)(2,1)S(1)}, bf16[8,2,128,256]{3,2,1,0:T(8,128)(2,1)S(1)}, u32[]{:S(2)}, u32[]{:S(2)}) collective-permute-start(bf16[8,2,128,256]{3,2,1,0:T(8,128)(2,1)S(1)} %all-to-all-done.2.refs_0_), channel_id=1, source_target_pairs={{0,8},{8,0},{1,9},{9,1},{2,10},{10,2},{3,11},{11,3},{4,12},{12,4},... | collective-permute-start | bytes 3145736 | tf_op jit(solution)/shard_map/ppermute | solution.py:189
  172.9 23.4 %collective-permute-start.3 = (bf16[4,2,128,256]{3,2,1,0:T(8,128)(2,1)S(1)}, bf16[4,2,128,256]{3,2,1,0:T(8,128)(2,1)S(1)}, u32[]{:S(2)}, u32[]{:S(2)}) collective-permute-start(bf16[4,2,128,256]{3,2,1,0:T(8,128)(2,1)S(1)} %get-tuple-element.10), channel_id=1, source_target_pairs={{0,48},{16,0},{32,16},{48,32},{1,49},{17,1},{33,17},{49,33},{2,50}... | collective-permute-start | bytes 1572872 | tf_op jit(solution)/shard_map/ppermute | solution.py:189
  173.6 22.7 %collective-permute-start.5 = (bf16[4,2,128,256]{3,2,1,0:T(8,128)(2,1)S(1)}, bf16[4,2,128,256]{3,2,1,0:T(8,128)(2,1)S(1)}, u32[]{:S(2)}, u32[]{:S(2)}) collective-permute-start(bf16[4,2,128,256]{3,2,1,0:T(8,128)(2,1)S(1)} %collective-permute-done.1.refs_1_), channel_id=1, source_target_pairs={{0,16},{16,32},{32,48},{48,0},{1,17},{17,33},{33,49},{49,1},{2,18}... | collective-permute-start | bytes 1572872 | tf_op jit(solution)/shard_map/ppermute | solution.py:189
  185.1 21.9 %collective-permute-start.6 = (bf16[4,2,128,256]{3,2,1,0:T(8,128)(2,1)S(1)}, bf16[4,2,128,256]{3,2,1,0:T(8,128)(2,1)S(1)}, u32[]{:S(2)}, u32[]{:S(2)}) collective-permute-start(bf16[4,2,128,256]{3,2,1,0:T(8,128)(2,1)S(1)} %collective-permute-done.4.refs_4_), channel_id=1, source_target_pairs={{0,48},{16,0},{32,16},{48,32},{1,49},{17,1},{33,17},{49,33},{2,50}... | collective-permute-start | bytes 1572872 | tf_op jit(solution)/shard_map/ppermute | solution.py:189
  196.3 11.2 %collective-permute-start.8 = (bf16[4,2,128,256]{3,2,1,0:T(8,128)(2,1)S(1)}, bf16[4,2,128,256]{3,2,1,0:T(8,128)(2,1)S(1)}, u32[]{:S(2)}, u32[]{:S(2)}) collective-permute-start(bf16[4,2,128,256]{3,2,1,0:T(8,128)(2,1)S(1)} %collective-permute-done.1.refs_1_), channel_id=1, source_target_pairs={{0,8},{8,0},{1,9},{9,1},{2,10},{10,2},{3,11},{11,3},{4,12},{12,4},... | collective-permute-start | bytes 1572872 | tf_op jit(solution)/shard_map/ppermute | solution.py:189
  196.3 11.3 %collective-permute-start.9 = (bf16[4,2,128,256]{3,2,1,0:T(8,128)(2,1)S(1)}, bf16[4,2,128,256]{3,2,1,0:T(8,128)(2,1)S(1)}, u32[]{:S(2)}, u32[]{:S(2)}) collective-permute-start(bf16[4,2,128,256]{3,2,1,0:T(8,128)(2,1)S(1)} %collective-permute-done.2.refs_2_), channel_id=1, source_target_pairs={{0,8},{8,0},{1,9},{9,1},{2,10},{10,2},{3,11},{11,3},{4,12},{12,4},... | collective-permute-start | bytes 1572872 | tf_op jit(solution)/shard_map/ppermute | solution.py:189
  207.0 2.7 collective-permute-start.11
  207.0 2.7 collective-permute-start.10
  207.5 2.9 %collective-permute-start.12 = (bf16[4,2,128,256]{3,2,1,0:T(8,128)(2,1)S(1)}, bf16[4,2,128,256]{3,2,1,0:T(8,128)(2,1)S(1)}, u32[]{:S(2)}, u32[]{:S(2)}) collective-permute-start(bf16[4,2,128,256]{3,2,1,0:T(8,128)(2,1)S(1)} %collective-permute-done.5.refs_5_), channel_id=1, source_target_pairs={{0,8},{8,0},{1,9},{9,1},{2,10},{10,2},{3,11},{11,3},{4,12},{12,4},... | collective-permute-start | bytes 1572872 | tf_op jit(solution)/shard_map/ppermute | solution.py:189
  207.6 3.6 %collective-permute-start.13 = (bf16[4,2,128,256]{3,2,1,0:T(8,128)(2,1)S(1)}, bf16[4,2,128,256]{3,2,1,0:T(8,128)(2,1)S(1)}, u32[]{:S(2)}, u32[]{:S(2)}) collective-permute-start(bf16[4,2,128,256]{3,2,1,0:T(8,128)(2,1)S(1)} %collective-permute-done.6.refs_6_), channel_id=1, source_target_pairs={{0,8},{8,0},{1,9},{9,1},{2,10},{10,2},{3,11},{11,3},{4,12},{12,4},... | collective-permute-start | bytes 1572872 | tf_op jit(solution)/shard_map/ppermute | solution.py:189

commit v4 on v3

--- a/solution.py
+++ b/solution.py
@@ -6,7 +6,6 @@
 from jax.sharding import Mesh, PartitionSpec as P
 
 CAP = 2
-CHUNKS = 4
 ROOM = 24 * 2**20
 ALL = ("ylo", "z", "core", "x", "yhi")
 COL = ("x", "yhi")
@@ -52,34 +51,46 @@
     return high, low
 
 
+def fetch_rotate_kernel(
+    core, slots, weights, arrived, left, right, out, held, left_v, right_v, sem_left, sem_right, sem
+):
+    copy = pltpu.make_async_copy(arrived, held, sem)
+    copy.start()
+    rotate_kernel(
+        core, slots, weights, held, left, right, out, left_v, right_v, sem_left, sem_right, copy
+    )
+
+
 def rotate_kernel(
-    core, slots, weights, arrived, left, right, mine, theirs, left_v, right_v, sem_left, sem_right
+    core, slots, weights, arrived, left, right, out, left_v, right_v, sem_left, sem_right, first=None
 ):
-    blocks = left.shape[0]
-    span = blocks // CHUNKS
+    groups = out.shape[0] // 8
     copies = []
-    for n in range(CHUNKS):
-        part = pl.ds(n * span, span)
+    for g in range(groups):
+        held = pl.ds(g * 16 + core[0] * 8, 8)
+        part = pl.ds(g * 8, 8)
         pair = (
-            pltpu.make_async_copy(left.at[part], left_v.at[part], sem_left.at[n]),
-            pltpu.make_async_copy(right.at[part], right_v.at[part], sem_right.at[n]),
+            pltpu.make_async_copy(left.at[held], left_v.at[part], sem_left.at[g]),
+            pltpu.make_async_copy(right.at[held], right_v.at[part], sem_right.at[g]),
         )
         for copy in pair:
             copy.start()
         copies.append(pair)
-
-    def block(f, out, place):
+    if first is not None:
+        first.wait()
+
+    def block(f, place):
         r = f * 4
         merged = weights[r] * arrived[slots[r]].astype(jnp.float32)
         for j in range(1, 4):
             merged += weights[r + j] * arrived[slots[r + j]].astype(jnp.float32)
-        lhs = left_v[f]
+        lhs = left_v[place]
         turned = jnp.dot(
             jnp.concatenate([lhs, lhs], axis=1),
             jnp.concatenate(split(merged), axis=0),
             preferred_element_type=jnp.float32,
         )
-        rhs = right_v[f]
+        rhs = right_v[place]
         fine = lax.dot_general(
             jnp.concatenate(split(turned), axis=1),
             jnp.concatenate([rhs, rhs], axis=1),
@@ -88,42 +99,38 @@
         )
         out[place] = fine.astype(jnp.bfloat16)
 
-    for n in range(CHUNKS):
-        for copy in copies[n]:
+    for g in range(0, groups, 2):
+        for copy in copies[g] + copies[g + 1]:
             copy.wait()
-
-        def several(i, carry):
-            group = n * (span // 16) + i
-            for k in range(8):
-                block(group * 16 + core[0] * 8 + k, mine, group * 8 + k)
-                block(group * 16 + (1 - core[0]) * 8 + k, theirs, group * 8 + k)
-            return carry
-
-        lax.fori_loop(0, span // 16, several, 0)
-
-
-def rotate(core, slots, weights, arrived, left, right):
-    half = jax.ShapeDtypeStruct((left.shape[0] // 2,) + left.shape[1:], jnp.bfloat16)
-    anywhere = pl.BlockSpec(memory_space=pl.ANY)
+        for k in range(16):
+            block((g + k // 8) * 16 + core[0] * 8 + k % 8, g * 8 + k)
+
+
+def rotate(core, slots, weights, arrived, left, right, fetch):
+    half = (left.shape[0] // 2,) + left.shape[1:]
+    anywhere = pl.BlockSpec(memory_space=pltpu.HBM)
     local = pl.BlockSpec(memory_space=pltpu.VMEM)
+    out = jax.ShapeDtypeStruct(half, jnp.bfloat16)
+    sems = pltpu.SemaphoreType.DMA((half[0] // 8,))
     return pl.pallas_call(
-        rotate_kernel,
+        fetch_rotate_kernel if fetch else rotate_kernel,
         grid_spec=pltpu.PrefetchScalarGridSpec(
             num_scalar_prefetch=3,
             grid=(),
-            in_specs=[local, anywhere, anywhere],
-            out_specs=[local, local],
+            in_specs=[anywhere if fetch else local, anywhere, anywhere],
+            out_specs=[local, local] if fetch else local,
             scratch_shapes=[
-                pltpu.VMEM(left.shape, jnp.bfloat16),
-                pltpu.VMEM(left.shape, jnp.bfloat16),
-                pltpu.SemaphoreType.DMA((CHUNKS,)),
-                pltpu.SemaphoreType.DMA((CHUNKS,)),
-            ],
-        ),
-        out_shape=[half, half],
+                pltpu.VMEM(half, jnp.bfloat16),
+                pltpu.VMEM(half, jnp.bfloat16),
+                sems,
+                sems,
+            ]
+            + [pltpu.SemaphoreType.DMA] * fetch,
+        ),
+        out_shape=[out, pltpu.VMEM(arrived.shape, arrived.dtype)] if fetch else out,
         compiler_params=pltpu.CompilerParams(vmem_limit_bytes=ROOM),
         name="rotate",
-    )(core, slots, weights, arrived, far(left), far(right))
+    )(core, slots, weights, far(arrived) if fetch else arrived, far(left), far(right))
 
 
 def panel_kernel(place, mine, other, *refs):
@@ -228,16 +235,16 @@
     ).astype(jnp.int32)
     wanted = jnp.sum(picker * jnp.arange(coarse_per, dtype=jnp.int32)[None, :, None], axis=1)
     requested = lax.all_to_all(wanted, ALL, split_axis=0, concat_axis=0, tiled=True)
-    served = serve(requested.reshape(-1), coarse_kernel).reshape(
-        (dev_count, CAP) + coarse_kernel.shape[1:]
-    )
+    served = serve(requested.reshape(-1), coarse_kernel)
+    served = served.reshape((dev_count, CAP) + coarse_kernel.shape[1:])
     arrived = lax.all_to_all(served, ALL, split_axis=0, concat_axis=0, tiled=True)
     arrived = arrived.reshape((dev_count * CAP,) + coarse_kernel.shape[1:])
     slot_table = (jnp.arange(dev_count, dtype=jnp.int32)[:, None] * CAP + slot_rank).reshape(-1)
     ref_slots = jnp.take(slot_table, ref_ids, mode="clip")
-    mine, theirs = rotate(
-        core.reshape(1), ref_slots, interp_weight.reshape(-1), arrived, left_rot, right_rot
-    )
+    weights = interp_weight.reshape(-1)
+    rots = left_rot, right_rot
+    theirs, held = rotate((1 - core).reshape(1), ref_slots, weights, arrived, *rots, True)
+    mine = rotate(core.reshape(1), ref_slots, weights, held, *rots, False)
     other = shift(theirs, "core", 1)
     partial_product = panel_product(place, mine, other, pieces)
     groups, parts, size, width = partial_product.shape

time: 286 us -> 276 us (0.965)
  waiting for transfers between devices: 147 us -> 140 us
  blocking collectives: 62 us -> 58.7 us
    ppermute x14, waiting for transfers between devices: 30.9 us -> 25 us  [shift(): lax.ppermute(value, axis, [(i, (i + step) % count) for i in range(count)])]
    all_to_all x1, blocking collectives: 62 us -> 58.7 us  [shards(): lax.all_to_all(partial_product.reshape(groups * parts, size, width), SAME...]
    pallas_call x1 -> x2, Pallas kernels: 12.6 us -> 14.2 us  [rotate(): pl.pallas_call(fetch_rotate_kernel if fetch else rotate_kernel, grid_spec...]
  transfers between devices with their start and end apart: 17 -> 17, of which waited for: 9 -> 8; matrix products, arithmetic and copies ran while one was open for 3% -> 3% of each run, Pallas kernels for 6% -> 7%
where the time goes in v4:
time: 276 us; the launch traced here: 275 us
  waiting for transfers between devices  140 us (51%)
  blocking collectives  58.7 us (21%)
  starting transfers between devices  32.9 us (12%)
  Pallas kernels  29.8 us (11%)
  local copies, waits for them, and re-layouts  8.22 us (3%)
  other arithmetic  4.63 us (2%)
    all_to_all x1, waiting for transfers between devices, shards(): lax.all_to_all(served, ALL, split_axis=0, concat_axis=0, tiled=True)  99.9 us
    all_to_all x1, blocking collectives, shards(): lax.all_to_all(partial_product.reshape(groups * parts, size, width), SAME...  58.7 us
    ppermute x14, waiting for transfers between devices, shift(): lax.ppermute(value, axis, [(i, (i + step) % count) for i in range(count)])  25 us
    pallas_call x2, Pallas kernels, rotate(): pl.pallas_call(fetch_rotate_kernel if fetch else rotate_kernel, grid_spec...  14.2 us
    ppermute x14, starting transfers between devices, shift(): lax.ppermute(value, axis, [(i, (i + step) % count) for i in range(count)])  11.7 us
    all_to_all x1, starting transfers between devices, shards(): lax.all_to_all(wanted, ALL, split_axis=0, concat_axis=0, tiled=True)  11.2 us
    pallas_call x1, Pallas kernels, panel_product(): pl.pallas_call(panel_kernel, grid_spec=pltpu.PrefetchScalarGridSpec(num_s...  10.6 us
    all_to_all x1, waiting for transfers between devices, trial_pieces(): own = lax.all_to_all(piece, COL, split_axis=0, concat_axis=0, tiled=True)  8.53 us
  transfers between devices with their start and end apart: 17, of which 8 were waited for; matrix products, arithmetic and copies ran while one was open for 3% of the time, Pallas kernels for 7%

profile of v4, /device:TPU:0, one launch (start us, length us, event | category | flops | bytes accessed | tf_op | source)
XLA Modules:
  0.0 274.7 jit_solution(331040921520348373)
XLA Ops:
  2.6 11.2 %all-to-all-start = ((s32[128,1,2]{2,1,0:T(1,128)}), s32[128,1,2]{2,1,0:T(1,128)S(1)}, u32[]{:S(2)}, u32[]{:S(2)}) async-start(s32[128,1,2]{2,1,0:T(1,128)} %copy.31), calls=%async_computation | async-start | bytes 131072 | tf_op jit(solution)/shard_map/all_to_all | solution.py:237
  13.8 1.3 constant_dynamic-slice_fusion
  15.2 1.2 fusion.1
  16.4 6.8 %all-to-all-done = s32[128,1,2]{2,1,0:T(1,128)S(1)} async-done(((s32[128,1,2]{2,1,0:T(1,128)}), s32[128,1,2]{2,1,0:T(1,128)S(1)}, u32[]{:S(2)}, u32[]{:S(2)}) %all-to-all-start) | async-done | bytes 1056 | tf_op jit(solution)/shard_map/all_to_all | solution.py:237
  23.2 3.6 %all-to-all-start.2 = ((bf16[8,2,128,256]{3,2,1,0:T(8,128)(2,1)}), bf16[8,2,128,256]{3,2,1,0:T(8,128)(2,1)S(1)}, u32[]{:S(2)}, u32[]{:S(2)}) async-start(bf16[8,2,128,256]{3,2,1,0:T(8,128)(2,1)} %fusion.1), calls=%async_computation.2 | async-start | bytes 2097152 | tf_op jit(solution)/shard_map/all_to_all | solution.py:208
  27.4 0.8 reduce.3
  28.9 5.0 %serve.1 = bf16[256,128,128]{2,1,0:T(8,128)(2,1)} custom-call(s32[256]{0:T(256)} %reshape.59.wanted, bf16[16,128,128]{2,1,0:T(8,128)(2,1)} %coarse.1), custom_call_target="tpu_custom_call" | custom-call | tf_op jit(solution)/shard_map/serve/pallas_call | solution.py:26
  33.9 8.5 %all-to-all-done.2.refs_0_ = bf16[8,2,128,256]{3,2,1,0:T(8,128)(2,1)S(1)} async-done(((bf16[8,2,128,256]{3,2,1,0:T(8,128)(2,1)}), bf16[8,2,128,256]{3,2,1,0:T(8,128)(2,1)S(1)}, u32[]{:S(2)}, u32[]{:S(2)}) %all-to-all-start.2) | async-done | bytes 1048608 | tf_op jit(solution)/shard_map/all_to_all | solution.py:208
  42.5 6.5 %all-to-all-start.1 = ((bf16[128,2,128,128]{3,2,1,0:T(8,128)(2,1)}), bf16[128,2,128,128]{3,2,1,0:T(8,128)(2,1)}, u32[]{:S(2)}, u32[]{:S(2)}) async-start(bf16[128,2,128,128]{3,2,1,0:T(8,128)(2,1)} %bitcast.14), calls=%async_computation.1 | async-start | bytes 16777216 | tf_op jit(solution)/shard_map/all_to_all | solution.py:240
  49.5 3.1 %gather_fusion = s32[512]{0:T(512)S(1)} fusion(s32[2048]{0:T(1024)S(1)} %subtract_add_fusion, s32[1024]{0:T(1024)S(1)} %pad_clamp_fusion), kind=kCustom, calls=%fused_computation | custom fusion | bytes 6144 | tf_op jit(solution)/shard_map/jit(_take)/gather | solution.py:243
  52.8 1.1 collective-permute-start.1
  53.9 2.2 collective-permute-start.4
  56.1 99.9 %all-to-all-done.1 = bf16[128,2,128,128]{3,2,1,0:T(8,128)(2,1)} async-done(((bf16[128,2,128,128]{3,2,1,0:T(8,128)(2,1)}), bf16[128,2,128,128]{3,2,1,0:T(8,128)(2,1)}, u32[]{:S(2)}, u32[]{:S(2)}) %all-to-all-start.1) | async-done | bytes 8388640 | tf_op jit(solution)/shard_map/all_to_all | solution.py:240
  156.0 8.8 %rotate.2 = (bf16[64,128,128]{2,1,0:T(8,128)(2,1)S(1)}, bf16[256,128,128]{2,1,0:T(8,128)(2,1)S(1)}) custom-call(s32[1]{0:T(128)} %bitcast.2.core, s32[512]{0:T(512)S(1)} %gather_fusion, f32[512]{0:T(512)S(1)} %reshape.57.weights, bf16[256,128,128]{2,1,0:T(8,128)(2,1)} %bitcast.5.arrived, bf16[128,128,128]{2,1,0:T(8,128)(2,1)} %left.3, ...), custom_call_target="tpu_custom_call" | custom-call | tf_op jit(solution)/shard_map/rotate/pallas_call | solution.py:115
  164.9 4.1 %collective-permute-start.3 = (bf16[4,2,128,256]{3,2,1,0:T(8,128)(2,1)S(1)}, bf16[4,2,128,256]{3,2,1,0:T(8,128)(2,1)S(1)}, u32[]{:S(2)}, u32[]{:S(2)}) collective-permute-start(bf16[4,2,128,256]{3,2,1,0:T(8,128)(2,1)S(1)} %get-tuple-element.10), channel_id=1, source_target_pairs={{0,48},{16,0},{32,16},{48,32},{1,49},{17,1},{33,17},{49,33},{2,50}... | collective-permute-start | bytes 1572872 | tf_op jit(solution)/shard_map/ppermute | solution.py:196
  169.2 3.0 %collective-permute-start.6 = (bf16[4,2,128,256]{3,2,1,0:T(8,128)(2,1)S(1)}, bf16[4,2,128,256]{3,2,1,0:T(8,128)(2,1)S(1)}, u32[]{:S(2)}, u32[]{:S(2)}) collective-permute-start(bf16[4,2,128,256]{3,2,1,0:T(8,128)(2,1)S(1)} %collective-permute-done.4.refs_4_), channel_id=1, source_target_pairs={{0,48},{16,0},{32,16},{48,32},{1,49},{17,1},{33,17},{49,33},{2,50}... | collective-permute-start | bytes 1572872 | tf_op jit(solution)/shard_map/ppermute | solution.py:196
  172.3 9.0 %collective-permute-done.3.refs_3_ = bf16[4,2,128,256]{3,2,1,0:T(8,128)(2,1)S(1)} collective-permute-done((bf16[4,2,128,256]{3,2,1,0:T(8,128)(2,1)S(1)}, bf16[4,2,128,256]{3,2,1,0:T(8,128)(2,1)S(1)}, u32[]{:S(2)}, u32[]{:S(2)}) %collective-permute-start.3) | collective-permute-done | bytes 524320 | tf_op jit(solution)/shard_map/ppermute | solution.py:196
  181.3 3.7 %collective-permute-done.2.refs_2_ = bf16[4,2,128,256]{3,2,1,0:T(8,128)(2,1)S(1)} collective-permute-done((bf16[4,2,128,256]{3,2,1,0:T(8,128)(2,1)S(1)}, bf16[4,2,128,256]{3,2,1,0:T(8,128)(2,1)S(1)}, u32[]{:S(2)}, u32[]{:S(2)}) %collective-permute-start.2) | collective-permute-done | bytes 524320 | tf_op jit(solution)/shard_map/ppermute | solution.py:196
  185.0 10.4 %collective-permute-done.5.refs_5_ = bf16[4,2,128,256]{3,2,1,0:T(8,128)(2,1)S(1)} collective-permute-done((bf16[4,2,128,256]{3,2,1,0:T(8,128)(2,1)S(1)}, bf16[4,2,128,256]{3,2,1,0:T(8,128)(2,1)S(1)}, u32[]{:S(2)}, u32[]{:S(2)}) %collective-permute-start.5) | collective-permute-done | bytes 524320 | tf_op jit(solution)/shard_map/ppermute | solution.py:196
  196.0 1.3 collective-permute-done.8.refs_8_
  198.2 5.4 %rotate.3.mine = bf16[64,128,128]{2,1,0:T(8,128)(2,1)S(1)} custom-call(s32[1]{0:T(128)} %bitcast.1.core, s32[512]{0:T(512)S(1)} %gather_fusion, f32[512]{0:T(512)S(1)} %reshape.57.weights, bf16[256,128,128]{2,1,0:T(8,128)(2,1)S(1)} %get-tuple-element.7.arrived, bf16[128,128,128]{2,1,0:T(8,128)(2,1)} %left.3, bf16[128,128,128]{2,1,0:T(8,128)(2,1)} %right.3), custom_call_target="tpu_custom_call" | custom-call | tf_op jit(solution)/shard_map/rotate/pallas_call | solution.py:115
  203.7 10.6 %panel.1 = bf16[8,8,128,256]{3,2,1,0:T(8,128)(2,1)} custom-call(s32[2]{0:T(128)S(1)} %pad_add_fusion.place, bf16[64,128,128]{2,1,0:T(8,128)(2,1)S(1)} %rotate.3.mine, bf16[64,128,128]{2,1,0:T(8,128)(2,1)S(1)} %collective-permute-done.other, bf16[8,2,128,256]{3,2,1,0:T(8,128)(2,1)S(1)} %all-to-all-done.2.refs_0_, ...), custom_call_target="tpu_custom_call" | custom-call | tf_op jit(solution)/shard_map/panel/pallas_call | solution.py:176
  214.3 58.7 %all_to_all.24 = bf16[64,128,256]{2,1,0:T(8,128)(2,1)S(1)} all-to-all(bf16[64,128,256]{2,1,0:T(8,128)(2,1)} %bitcast.15), channel_id=1, replica_groups=mesh['ylo'=2,'z'=4,'core'=2,'x'=4,'yhi'=2] {'ylo','z','x','yhi'}, dimensions={0} | all-to-all | bytes 8388608 | tf_op jit(solution)/shard_map/all_to_all | solution.py:251
  273.0 1.7 convert_reduce_fusion
  (46 shorter events, 6.6 us)
Async XLA Ops:
  2.6 20.6 %all-to-all-start = ((s32[128,1,2]{2,1,0:T(1,128)}), s32[128,1,2]{2,1,0:T(1,128)S(1)}, u32[]{:S(2)}, u32[]{:S(2)}) async-start(s32[128,1,2]{2,1,0:T(1,128)} %copy.31), calls=%async_computation | async-start | bytes 131072 | tf_op jit(solution)/shard_map/all_to_all | solution.py:237
  23.2 19.2 %all-to-all-start.2 = ((bf16[8,2,128,256]{3,2,1,0:T(8,128)(2,1)}), bf16[8,2,128,256]{3,2,1,0:T(8,128)(2,1)S(1)}, u32[]{:S(2)}, u32[]{:S(2)}) async-start(bf16[8,2,128,256]{3,2,1,0:T(8,128)(2,1)} %fusion.1), calls=%async_computation.2 | async-start | bytes 2097152 | tf_op jit(solution)/shard_map/all_to_all | solution.py:208
  42.5 6.8 %copy-start = (f32[128,4]{0,1:T(4,128)S(1)}, f32[128,4]{0,1:T(4,128)}, u32[]{:S(2)}) copy-start(f32[128,4]{0,1:T(4,128)} %param.8) | copy-start | bytes 6148
  42.5 113.5 %all-to-all-start.1 = ((bf16[128,2,128,128]{3,2,1,0:T(8,128)(2,1)}), bf16[128,2,128,128]{3,2,1,0:T(8,128)(2,1)}, u32[]{:S(2)}, u32[]{:S(2)}) async-start(bf16[128,2,128,128]{3,2,1,0:T(8,128)(2,1)} %bitcast.14), calls=%async_computation.1 | async-start | bytes 16777216 | tf_op jit(solution)/shard_map/all_to_all | solution.py:240
  52.8 116.2 %collective-permute-start.1 = (bf16[4,2,128,256]{3,2,1,0:T(8,128)(2,1)S(1)}, bf16[4,2,128,256]{3,2,1,0:T(8,128)(2,1)S(1)}, u32[]{:S(2)}, u32[]{:S(2)}) collective-permute-start(bf16[4,2,128,256]{3,2,1,0:T(8,128)(2,1)S(1)} %get-tuple-element.10), channel_id=1, source_target_pairs={{0,16},{16,32},{32,48},{48,0},{1,17},{17,33},{33,49},{49,1},{2,18}... | collective-permute-start | bytes 1572872 | tf_op jit(solution)/shard_map/ppermute | solution.py:196
  53.9 115.4 %collective-permute-start.4 = (bf16[4,2,128,256]{3,2,1,0:T(8,128)(2,1)S(1)}, bf16[4,2,128,256]{3,2,1,0:T(8,128)(2,1)S(1)}, u32[]{:S(2)}, u32[]{:S(2)}) collective-permute-start(bf16[4,2,128,256]{3,2,1,0:T(8,128)(2,1)S(1)} %get-tuple-element.9), channel_id=1, source_target_pairs={{0,48},{16,0},{32,16},{48,32},{1,49},{17,1},{33,17},{49,33},{2,50}... | collective-permute-start | bytes 1572872 | tf_op jit(solution)/shard_map/ppermute | solution.py:196
  164.8 39.0 %collective-permute-start = (bf16[64,128,128]{2,1,0:T(8,128)(2,1)S(1)}, bf16[64,128,128]{2,1,0:T(8,128)(2,1)S(1)}, u32[]{:S(2)}, u32[]{:S(2)}) collective-permute-start(bf16[64,128,128]{2,1,0:T(8,128)(2,1)S(1)} %get-tuple-element.8), channel_id=1, source_target_pairs={{0,8},{8,0},{1,9},{9,1},{2,10},{10,2},{3,11},{11,3},{4,12},{12,4},... | collective-permute-start | bytes 6291464 | tf_op jit(solution)/shard_map/ppermute | solution.py:196
  164.9 16.4 %collective-permute-start.3 = (bf16[4,2,128,256]{3,2,1,0:T(8,128)(2,1)S(1)}, bf16[4,2,128,256]{3,2,1,0:T(8,128)(2,1)S(1)}, u32[]{:S(2)}, u32[]{:S(2)}) collective-permute-start(bf16[4,2,128,256]{3,2,1,0:T(8,128)(2,1)S(1)} %get-tuple-element.10), channel_id=1, source_target_pairs={{0,48},{16,0},{32,16},{48,32},{1,49},{17,1},{33,17},{49,33},{2,50}... | collective-permute-start | bytes 1572872 | tf_op jit(solution)/shard_map/ppermute | solution.py:196
  168.9 16.0 %collective-permute-start.2 = (bf16[4,2,128,256]{3,2,1,0:T(8,128)(2,1)S(1)}, bf16[4,2,128,256]{3,2,1,0:T(8,128)(2,1)S(1)}, u32[]{:S(2)}, u32[]{:S(2)}) collective-permute-start(bf16[4,2,128,256]{3,2,1,0:T(8,128)(2,1)S(1)} %get-tuple-element.9), channel_id=1, source_target_pairs={{0,16},{16,32},{32,48},{48,0},{1,17},{17,33},{33,49},{49,1},{2,18}... | collective-permute-start | bytes 1572872 | tf_op jit(solution)/shard_map/ppermute | solution.py:196
  168.9 26.4 %collective-permute-start.5 = (bf16[4,2,128,256]{3,2,1,0:T(8,128)(2,1)S(1)}, bf16[4,2,128,256]{3,2,1,0:T(8,128)(2,1)S(1)}, u32[]{:S(2)}, u32[]{:S(2)}) collective-permute-start(bf16[4,2,128,256]{3,2,1,0:T(8,128)(2,1)S(1)} %collective-permute-done.1.refs_1_), channel_id=1, source_target_pairs={{0,16},{16,32},{32,48},{48,0},{1,17},{17,33},{33,49},{49,1},{2,18}... | collective-permute-start | bytes 1572872 | tf_op jit(solution)/shard_map/ppermute | solution.py:196
  169.2 26.1 %collective-permute-start.6 = (bf16[4,2,128,256]{3,2,1,0:T(8,128)(2,1)S(1)}, bf16[4,2,128,256]{3,2,1,0:T(8,128)(2,1)S(1)}, u32[]{:S(2)}, u32[]{:S(2)}) collective-permute-start(bf16[4,2,128,256]{3,2,1,0:T(8,128)(2,1)S(1)} %collective-permute-done.4.refs_4_), channel_id=1, source_target_pairs={{0,48},{16,0},{32,16},{48,32},{1,49},{17,1},{33,17},{49,33},{2,50}... | collective-permute-start | bytes 1572872 | tf_op jit(solution)/shard_map/ppermute | solution.py:196
  181.3 22.4 %collective-permute-start.7 = (bf16[8,2,128,256]{3,2,1,0:T(8,128)(2,1)S(1)}, bf16[8,2,128,256]{3,2,1,0:T(8,128)(2,1)S(1)}, u32[]{:S(2)}, u32[]{:S(2)}) collective-permute-start(bf16[8,2,128,256]{3,2,1,0:T(8,128)(2,1)S(1)} %all-to-all-done.2.refs_0_), channel_id=1, source_target_pairs={{0,8},{8,0},{1,9},{9,1},{2,10},{10,2},{3,11},{11,3},{4,12},{12,4},... | collective-permute-start | bytes 3145736 | tf_op jit(solution)/shard_map/ppermute | solution.py:196
  184.9 10.9 %collective-permute-start.11 = (bf16[4,2,128,256]{3,2,1,0:T(8,128)(2,1)S(1)}, bf16[4,2,128,256]{3,2,1,0:T(8,128)(2,1)S(1)}, u32[]{:S(2)}, u32[]{:S(2)}) collective-permute-start(bf16[4,2,128,256]{3,2,1,0:T(8,128)(2,1)S(1)} %collective-permute-done.4.refs_4_), channel_id=1, source_target_pairs={{0,8},{8,0},{1,9},{9,1},{2,10},{10,2},{3,11},{11,3},{4,12},{12,4},... | collective-permute-start | bytes 1572872 | tf_op jit(solution)/shard_map/ppermute | solution.py:196
  195.4 1.9 collective-permute-start.8
  195.4 2.7 collective-permute-start.10
  195.9 7.8 %collective-permute-start.9 = (bf16[4,2,128,256]{3,2,1,0:T(8,128)(2,1)S(1)}, bf16[4,2,128,256]{3,2,1,0:T(8,128)(2,1)S(1)}, u32[]{:S(2)}, u32[]{:S(2)}) collective-permute-start(bf16[4,2,128,256]{3,2,1,0:T(8,128)(2,1)S(1)} %collective-permute-done.2.refs_2_), channel_id=1, source_target_pairs={{0,8},{8,0},{1,9},{9,1},{2,10},{10,2},{3,11},{11,3},{4,12},{12,4},... | collective-permute-start | bytes 1572872 | tf_op jit(solution)/shard_map/ppermute | solution.py:196
  197.3 6.4 %collective-permute-start.12 = (bf16[4,2,128,256]{3,2,1,0:T(8,128)(2,1)S(1)}, bf16[4,2,128,256]{3,2,1,0:T(8,128)(2,1)S(1)}, u32[]{:S(2)}, u32[]{:S(2)}) collective-permute-start(bf16[4,2,128,256]{3,2,1,0:T(8,128)(2,1)S(1)} %collective-permute-done.5.refs_5_), channel_id=1, source_target_pairs={{0,8},{8,0},{1,9},{9,1},{2,10},{10,2},{3,11},{11,3},{4,12},{12,4},... | collective-permute-start | bytes 1572872 | tf_op jit(solution)/shard_map/ppermute | solution.py:196
  198.0 5.7 %collective-permute-start.13 = (bf16[4,2,128,256]{3,2,1,0:T(8,128)(2,1)S(1)}, bf16[4,2,128,256]{3,2,1,0:T(8,128)(2,1)S(1)}, u32[]{:S(2)}, u32[]{:S(2)}) collective-permute-start(bf16[4,2,128,256]{3,2,1,0:T(8,128)(2,1)S(1)} %collective-permute-done.6.refs_6_), channel_id=1, source_target_pairs={{0,8},{8,0},{1,9},{9,1},{2,10},{10,2},{3,11},{11,3},{4,12},{12,4},... | collective-permute-start | bytes 1572872 | tf_op jit(solution)/shard_map/ppermute | solution.py:196

commit v5 on v4

--- a/solution.py
+++ b/solution.py
@@ -134,11 +134,11 @@
 
 
 def panel_kernel(place, mine, other, *refs):
-    pieces, out, out_v, sem = refs[:14], refs[14], refs[15], refs[16]
+    pieces, out, out_v, sem = refs[:16], refs[16], refs[17], refs[18]
     groups = mine.shape[0] // 8
     for side in range(2):
-        held = pieces[side * 7 : side * 7 + 7]
-        own, before, after, beyond = held[:1], held[1:3], held[3:5], held[5:]
+        held = pieces[side * 8 : side * 8 + 8]
+        own, before, after, beyond = held[:2], held[2:4], held[4:6], held[6:]
         order = (mine, other) if side == 0 else (other, mine)
         core = place[1] if side == 0 else 1 - place[1]
         for rel, parts in enumerate((own, after, beyond, before)):
@@ -156,7 +156,15 @@
                 ],
                 axis=0,
             )
-            rhs = jnp.concatenate([p[...].reshape(-1, p.shape[-1]) for p in parts], axis=0)
+            near_half, far_half = [p[...].reshape(-1, p.shape[-1]) for p in parts]
+            first = place[2] == 0
+            rhs = jnp.concatenate(
+                [
+                    jnp.where(first, near_half, far_half),
+                    jnp.where(first, far_half, near_half),
+                ],
+                axis=1,
+            )
             slot = side * 4 + rel
             out_v[slot] = (
                 jnp.dot(lhs, rhs, preferred_element_type=jnp.float32)
@@ -171,7 +179,7 @@
 def panel_product(place, mine, other, pieces):
     groups = mine.shape[0] // 8
     size = mine.shape[1]
-    width = pieces[0].shape[-1]
+    width = pieces[0].shape[-1] * 2
     local = pl.BlockSpec(memory_space=pltpu.VMEM)
     return pl.pallas_call(
         panel_kernel,
@@ -197,30 +205,32 @@
 
 
 def trial_pieces(trial):
+    ylo = lax.axis_index("ylo")
     z = lax.axis_index("z")
     core = lax.axis_index("core")
     rows, wide = trial.shape
-    width = wide // 8
-    piece = lax.dynamic_slice_in_dim(trial, (z * 2 + core) * width, width, axis=1)
+    width = wide // 16
+    piece = lax.dynamic_slice_in_dim(trial, ((z * 2 + core) * 2 + ylo) * width, width, axis=1)
     piece = piece.reshape(2, 8, rows // 16, width)
     piece = jnp.where(core == 0, piece, piece[::-1])
     piece = jnp.transpose(piece, (1, 0, 2, 3))
     own = lax.all_to_all(piece, COL, split_axis=0, concat_axis=0, tiled=True)
-    halves = own[:4], own[4:]
-    before = [shift(half, "z", 1) for half in halves]
-    after = [shift(half, "z", -1) for half in halves]
+    twin = shift(own, "ylo", 1)
+    before, after = [shift(own, "z", 1)], [shift(own, "z", -1)]
+    before.append(shift(twin, "z", 1))
+    after.append(shift(twin, "z", -1))
     top = shift(before[0], "z", 1)
-    bottom = shift(after[1], "z", -1)
-    early = [shift(value, "core", 1) for value in (own, *before, *after)]
+    bottom = shift(top, "ylo", 1)
+    early = [shift(value, "core", 1) for value in (own, twin, *before, *after)]
     late = [shift(value, "core", 1) for value in (top, bottom)]
-    return (own, *before, *after, top, bottom, *early, *late)
+    return (own, twin, *before, *after, top, bottom, *early, *late)
 
 
 def shards(coarse_kernel, interp_index, interp_weight, left_rot, right_rot, trial):
     dev_count = lax.axis_size(ALL)
     core = lax.axis_index("core").astype(jnp.int32)
     coarse_per = coarse_kernel.shape[0]
-    place = jnp.stack([lax.axis_index("z").astype(jnp.int32), core])
+    place = jnp.stack([lax.axis_index(axis).astype(jnp.int32) for axis in ("z", "core", "ylo")])
     pieces = trial_pieces(trial)
     ref_ids = interp_index.reshape(-1)
     catalog = jnp.arange(dev_count * coarse_per, dtype=jnp.int32)

time: 276 us -> 281 us (1.018)
  waiting for transfers between devices: 140 us -> 144 us
    ppermute x14 -> x16, waiting for transfers between devices: 25 us -> 34.5 us  [shift(): lax.ppermute(value, axis, [(i, (i + step) % count) for i in range(count)])]
    all_to_all x1, waiting for transfers between devices: 8.53 us -> 3.69 us  [trial_pieces(): own = lax.all_to_all(piece, COL, split_axis=0, concat_axis=0, tiled=True)]
    ppermute x14 -> x16, starting transfers between devices: 11.7 us -> 11.2 us  [shift(): lax.ppermute(value, axis, [(i, (i + step) % count) for i in range(count)])]
  transfers between devices with their start and end apart: 17 -> 19, of which waited for: 8 -> 7; matrix products, arithmetic and copies ran while one was open for 3% -> 3% of each run, Pallas kernels for 7% -> 7%
where the time goes in v5:
time: 281 us; the launch traced here: 280 us
  waiting for transfers between devices  144 us (51%)
  blocking collectives  61.4 us (22%)
  starting transfers between devices  31.9 us (11%)
  Pallas kernels  29.8 us (11%)
  local copies, waits for them, and re-layouts  7.87 us (3%)
  other arithmetic  4.31 us (2%)
    all_to_all x1, waiting for transfers between devices, shards(): lax.all_to_all(served, ALL, split_axis=0, concat_axis=0, tiled=True)  98.9 us
    all_to_all x1, blocking collectives, shards(): lax.all_to_all(partial_product.reshape(groups * parts, size, width), SAME...  61.4 us
    ppermute x16, waiting for transfers between devices, shift(): lax.ppermute(value, axis, [(i, (i + step) % count) for i in range(count)])  34.5 us
    pallas_call x2, Pallas kernels, rotate(): pl.pallas_call(fetch_rotate_kernel if fetch else rotate_kernel, grid_spec...  14.2 us
    ppermute x16, starting transfers between devices, shift(): lax.ppermute(value, axis, [(i, (i + step) % count) for i in range(count)])  11.2 us
    all_to_all x1, starting transfers between devices, shards(): lax.all_to_all(wanted, ALL, split_axis=0, concat_axis=0, tiled=True)  11.2 us
    pallas_call x1, Pallas kernels, panel_product(): pl.pallas_call(panel_kernel, grid_spec=pltpu.PrefetchScalarGridSpec(num_s...  10.6 us
    all_to_all x1, waiting for transfers between devices, shards(): lax.all_to_all(wanted, ALL, split_axis=0, concat_axis=0, tiled=True)  7.32 us
  transfers between devices with their start and end apart: 19, of which 7 were waited for; matrix products, arithmetic and copies ran while one was open for 3% of the time, Pallas kernels for 7%

profile of v5, /device:TPU:0, one launch (start us, length us, event | category | flops | bytes accessed | tf_op | source)
XLA Modules:
  0.0 280.0 jit_solution(14261634752743809219)
XLA Ops:
  0.0 0.8 copy.25
  2.6 11.2 %all-to-all-start = ((s32[128,1,2]{2,1,0:T(1,128)}), s32[128,1,2]{2,1,0:T(1,128)S(1)}, u32[]{:S(2)}, u32[]{:S(2)}) async-start(s32[128,1,2]{2,1,0:T(1,128)} %copy.31), calls=%async_computation | async-start | bytes 131072 | tf_op jit(solution)/shard_map/all_to_all | solution.py:247
  13.8 1.1 constant_dynamic-slice_fusion
  14.9 0.9 fusion.1
  15.9 7.3 %all-to-all-done = s32[128,1,2]{2,1,0:T(1,128)S(1)} async-done(((s32[128,1,2]{2,1,0:T(1,128)}), s32[128,1,2]{2,1,0:T(1,128)S(1)}, u32[]{:S(2)}, u32[]{:S(2)}) %all-to-all-start) | async-done | bytes 1056 | tf_op jit(solution)/shard_map/all_to_all | solution.py:247
  23.2 3.5 %all-to-all-start.2 = ((bf16[8,2,128,128]{3,2,1,0:T(8,128)(2,1)}), bf16[8,2,128,128]{3,2,1,0:T(8,128)(2,1)S(1)}, u32[]{:S(2)}, u32[]{:S(2)}) async-start(bf16[8,2,128,128]{3,2,1,0:T(8,128)(2,1)} %fusion.1), calls=%async_computation.2 | async-start | bytes 1048576 | tf_op jit(solution)/shard_map/all_to_all | solution.py:217
  28.8 5.0 %serve.1 = bf16[256,128,128]{2,1,0:T(8,128)(2,1)} custom-call(s32[256]{0:T(256)} %reshape.59.wanted, bf16[16,128,128]{2,1,0:T(8,128)(2,1)} %coarse.1), custom_call_target="tpu_custom_call" | custom-call | tf_op jit(solution)/shard_map/serve/pallas_call | solution.py:26
  33.8 3.7 %all-to-all-done.2.refs_0_ = bf16[8,2,128,128]{3,2,1,0:T(8,128)(2,1)S(1)} async-done(((bf16[8,2,128,128]{3,2,1,0:T(8,128)(2,1)}), bf16[8,2,128,128]{3,2,1,0:T(8,128)(2,1)S(1)}, u32[]{:S(2)}, u32[]{:S(2)}) %all-to-all-start.2) | async-done | bytes 524320 | tf_op jit(solution)/shard_map/all_to_all | solution.py:217
  37.4 6.1 %all-to-all-start.1 = ((bf16[128,2,128,128]{3,2,1,0:T(8,128)(2,1)}), bf16[128,2,128,128]{3,2,1,0:T(8,128)(2,1)}, u32[]{:S(2)}, u32[]{:S(2)}) async-start(bf16[128,2,128,128]{3,2,1,0:T(8,128)(2,1)} %bitcast.15), calls=%async_computation.1 | async-start | bytes 16777216 | tf_op jit(solution)/shard_map/all_to_all | solution.py:250
  44.1 3.1 %gather_fusion = s32[512]{0:T(512)S(1)} fusion(s32[2048]{0:T(1024)S(1)} %subtract_add_fusion, s32[1024]{0:T(1024)S(1)} %pad_clamp_fusion), kind=kCustom, calls=%fused_computation | custom fusion | bytes 6144 | tf_op jit(solution)/shard_map/jit(_take)/gather | solution.py:253
  47.3 0.9 collective-permute-start.1
  48.2 1.7 collective-permute-start.2
  49.9 1.8 collective-permute-start.4
  51.6 98.9 %all-to-all-done.1 = bf16[128,2,128,128]{3,2,1,0:T(8,128)(2,1)} async-done(((bf16[128,2,128,128]{3,2,1,0:T(8,128)(2,1)}), bf16[128,2,128,128]{3,2,1,0:T(8,128)(2,1)}, u32[]{:S(2)}, u32[]{:S(2)}) %all-to-all-start.1) | async-done | bytes 8388640 | tf_op jit(solution)/shard_map/all_to_all | solution.py:250
  150.6 8.8 %rotate.2 = (bf16[64,128,128]{2,1,0:T(8,128)(2,1)S(1)}, bf16[256,128,128]{2,1,0:T(8,128)(2,1)S(1)}) custom-call(s32[1]{0:T(128)} %bitcast.3.core, s32[512]{0:T(512)S(1)} %gather_fusion, f32[512]{0:T(512)S(1)} %reshape.57.weights, bf16[256,128,128]{2,1,0:T(8,128)(2,1)} %bitcast.6.arrived, bf16[128,128,128]{2,1,0:T(8,128)(2,1)} %left.3, ...), custom_call_target="tpu_custom_call" | custom-call | tf_op jit(solution)/shard_map/rotate/pallas_call | solution.py:115
  159.9 4.1 %collective-permute-start.5 = (bf16[8,2,128,128]{3,2,1,0:T(8,128)(2,1)S(1)}, bf16[8,2,128,128]{3,2,1,0:T(8,128)(2,1)S(1)}, u32[]{:S(2)}, u32[]{:S(2)}) collective-permute-start(bf16[8,2,128,128]{3,2,1,0:T(8,128)(2,1)S(1)} %collective-permute-done.1.refs_1_), channel_id=1, source_target_pairs={{0,48},{16,0},{32,16},{48,32},{1,49},{17,1},{33,17},{49,33},{2,50}... | collective-permute-start | bytes 1572872 | tf_op jit(solution)/shard_map/ppermute | solution.py:204
  164.5 12.2 %collective-permute-done.3.refs_3_ = bf16[8,2,128,128]{3,2,1,0:T(8,128)(2,1)S(1)} collective-permute-done((bf16[8,2,128,128]{3,2,1,0:T(8,128)(2,1)S(1)}, bf16[8,2,128,128]{3,2,1,0:T(8,128)(2,1)S(1)}, u32[]{:S(2)}, u32[]{:S(2)}) %collective-permute-start.3) | collective-permute-done | bytes 524320 | tf_op jit(solution)/shard_map/ppermute | solution.py:204
  177.2 10.1 %collective-permute-done.6.refs_6_ = bf16[8,2,128,128]{3,2,1,0:T(8,128)(2,1)S(1)} collective-permute-done((bf16[8,2,128,128]{3,2,1,0:T(8,128)(2,1)S(1)}, bf16[8,2,128,128]{3,2,1,0:T(8,128)(2,1)S(1)}, u32[]{:S(2)}, u32[]{:S(2)}) %collective-permute-start.6) | collective-permute-done | bytes 524320 | tf_op jit(solution)/shard_map/ppermute | solution.py:204
  187.4 0.9 collective-permute-start.7
  188.9 11.8 %collective-permute-done.7.refs_7_ = bf16[8,2,128,128]{3,2,1,0:T(8,128)(2,1)S(1)} collective-permute-done((bf16[8,2,128,128]{3,2,1,0:T(8,128)(2,1)S(1)}, bf16[8,2,128,128]{3,2,1,0:T(8,128)(2,1)S(1)}, u32[]{:S(2)}, u32[]{:S(2)}) %collective-permute-start.7) | collective-permute-done | bytes 524320 | tf_op jit(solution)/shard_map/ppermute | solution.py:204
  200.8 5.4 %rotate.3.mine = bf16[64,128,128]{2,1,0:T(8,128)(2,1)S(1)} custom-call(s32[1]{0:T(128)} %bitcast.1.core, s32[512]{0:T(512)S(1)} %gather_fusion, f32[512]{0:T(512)S(1)} %reshape.57.weights, bf16[256,128,128]{2,1,0:T(8,128)(2,1)S(1)} %get-tuple-element.7.arrived, bf16[128,128,128]{2,1,0:T(8,128)(2,1)} %left.3, bf16[128,128,128]{2,1,0:T(8,128)(2,1)} %right.3), custom_call_target="tpu_custom_call" | custom-call | tf_op jit(solution)/shard_map/rotate/pallas_call | solution.py:115
  206.3 10.6 %panel.1 = bf16[8,8,128,256]{3,2,1,0:T(8,128)(2,1)} custom-call(s32[3]{0:T(128)S(1)} %pad_add_fusion.place, bf16[64,128,128]{2,1,0:T(8,128)(2,1)S(1)} %rotate.3.mine, bf16[64,128,128]{2,1,0:T(8,128)(2,1)S(1)} %collective-permute-done.other, bf16[8,2,128,128]{3,2,1,0:T(8,128)(2,1)S(1)} %all-to-all-done.2.refs_0_, ...), custom_call_target="tpu_custom_call" | custom-call | tf_op jit(solution)/shard_map/panel/pallas_call | solution.py:184
  216.9 61.4 %all_to_all.24 = bf16[64,128,256]{2,1,0:T(8,128)(2,1)S(1)} all-to-all(bf16[64,128,256]{2,1,0:T(8,128)(2,1)} %bitcast.16), channel_id=1, replica_groups=mesh['ylo'=2,'z'=4,'core'=2,'x'=4,'yhi'=2] {'ylo','z','x','yhi'}, dimensions={0} | all-to-all | bytes 8388608 | tf_op jit(solution)/shard_map/all_to_all | solution.py:261
  278.3 1.7 convert_reduce_fusion
  (49 shorter events, 6.7 us)
Async XLA Ops:
  2.6 20.6 %all-to-all-start = ((s32[128,1,2]{2,1,0:T(1,128)}), s32[128,1,2]{2,1,0:T(1,128)S(1)}, u32[]{:S(2)}, u32[]{:S(2)}) async-start(s32[128,1,2]{2,1,0:T(1,128)} %copy.31), calls=%async_computation | async-start | bytes 131072 | tf_op jit(solution)/shard_map/all_to_all | solution.py:247
  23.2 14.2 %all-to-all-start.2 = ((bf16[8,2,128,128]{3,2,1,0:T(8,128)(2,1)}), bf16[8,2,128,128]{3,2,1,0:T(8,128)(2,1)S(1)}, u32[]{:S(2)}, u32[]{:S(2)}) async-start(bf16[8,2,128,128]{3,2,1,0:T(8,128)(2,1)} %fusion.1), calls=%async_computation.2 | async-start | bytes 1048576 | tf_op jit(solution)/shard_map/all_to_all | solution.py:217
  37.4 6.4 %copy-start = (f32[128,4]{0,1:T(4,128)S(1)}, f32[128,4]{0,1:T(4,128)}, u32[]{:S(2)}) copy-start(f32[128,4]{0,1:T(4,128)} %param.8) | copy-start | bytes 6148
  37.4 113.1 %all-to-all-start.1 = ((bf16[128,2,128,128]{3,2,1,0:T(8,128)(2,1)}), bf16[128,2,128,128]{3,2,1,0:T(8,128)(2,1)}, u32[]{:S(2)}, u32[]{:S(2)}) async-start(bf16[128,2,128,128]{3,2,1,0:T(8,128)(2,1)} %bitcast.15), calls=%async_computation.1 | async-start | bytes 16777216 | tf_op jit(solution)/shard_map/all_to_all | solution.py:250
  47.3 112.7 %collective-permute-start.1 = (bf16[8,2,128,128]{3,2,1,0:T(8,128)(2,1)S(1)}, bf16[8,2,128,128]{3,2,1,0:T(8,128)(2,1)S(1)}, u32[]{:S(2)}, u32[]{:S(2)}) collective-permute-start(bf16[8,2,128,128]{3,2,1,0:T(8,128)(2,1)S(1)} %all-to-all-done.2.refs_0_), channel_id=1, source_target_pairs={{0,64},{64,0},{1,65},{65,1},{2,66},{66,2},{3,67},{67,3},{4,68},{68... | collective-permute-start | bytes 1572872 | tf_op jit(solution)/shard_map/ppermute | solution.py:204
  48.2 111.8 %collective-permute-start.2 = (bf16[8,2,128,128]{3,2,1,0:T(8,128)(2,1)S(1)}, bf16[8,2,128,128]{3,2,1,0:T(8,128)(2,1)S(1)}, u32[]{:S(2)}, u32[]{:S(2)}) collective-permute-start(bf16[8,2,128,128]{3,2,1,0:T(8,128)(2,1)S(1)} %all-to-all-done.2.refs_0_), channel_id=1, source_target_pairs={{0,16},{16,32},{32,48},{48,0},{1,17},{17,33},{33,49},{49,1},{2,18}... | collective-permute-start | bytes 1572872 | tf_op jit(solution)/shard_map/ppermute | solution.py:204
  49.9 114.1 %collective-permute-start.4 = (bf16[8,2,128,128]{3,2,1,0:T(8,128)(2,1)S(1)}, bf16[8,2,128,128]{3,2,1,0:T(8,128)(2,1)S(1)}, u32[]{:S(2)}, u32[]{:S(2)}) collective-permute-start(bf16[8,2,128,128]{3,2,1,0:T(8,128)(2,1)S(1)} %all-to-all-done.2.refs_0_), channel_id=1, source_target_pairs={{0,48},{16,0},{32,16},{48,32},{1,49},{17,1},{33,17},{49,33},{2,50}... | collective-permute-start | bytes 1572872 | tf_op jit(solution)/shard_map/ppermute | solution.py:204
  159.3 46.9 %collective-permute-start = (bf16[64,128,128]{2,1,0:T(8,128)(2,1)S(1)}, bf16[64,128,128]{2,1,0:T(8,128)(2,1)S(1)}, u32[]{:S(2)}, u32[]{:S(2)}) collective-permute-start(bf16[64,128,128]{2,1,0:T(8,128)(2,1)S(1)} %get-tuple-element.8), channel_id=1, source_target_pairs={{0,8},{8,0},{1,9},{9,1},{2,10},{10,2},{3,11},{11,3},{4,12},{12,4},... | collective-permute-start | bytes 6291464 | tf_op jit(solution)/shard_map/ppermute | solution.py:204
  159.4 4.9 %collective-permute-start.8 = (bf16[8,2,128,128]{3,2,1,0:T(8,128)(2,1)S(1)}, bf16[8,2,128,128]{3,2,1,0:T(8,128)(2,1)S(1)}, u32[]{:S(2)}, u32[]{:S(2)}) collective-permute-start(bf16[8,2,128,128]{3,2,1,0:T(8,128)(2,1)S(1)} %all-to-all-done.2.refs_0_), channel_id=1, source_target_pairs={{0,8},{8,0},{1,9},{9,1},{2,10},{10,2},{3,11},{11,3},{4,12},{12,4},... | collective-permute-start | bytes 1572872 | tf_op jit(solution)/shard_map/ppermute | solution.py:204
  159.9 16.8 %collective-permute-start.3 = (bf16[8,2,128,128]{3,2,1,0:T(8,128)(2,1)S(1)}, bf16[8,2,128,128]{3,2,1,0:T(8,128)(2,1)S(1)}, u32[]{:S(2)}, u32[]{:S(2)}) collective-permute-start(bf16[8,2,128,128]{3,2,1,0:T(8,128)(2,1)S(1)} %collective-permute-done.1.refs_1_), channel_id=1, source_target_pairs={{0,16},{16,32},{32,48},{48,0},{1,17},{17,33},{33,49},{49,1},{2,18}... | collective-permute-start | bytes 1572872 | tf_op jit(solution)/shard_map/ppermute | solution.py:204
  159.9 16.8 %collective-permute-start.5 = (bf16[8,2,128,128]{3,2,1,0:T(8,128)(2,1)S(1)}, bf16[8,2,128,128]{3,2,1,0:T(8,128)(2,1)S(1)}, u32[]{:S(2)}, u32[]{:S(2)}) collective-permute-start(bf16[8,2,128,128]{3,2,1,0:T(8,128)(2,1)S(1)} %collective-permute-done.1.refs_1_), channel_id=1, source_target_pairs={{0,48},{16,0},{32,16},{48,32},{1,49},{17,1},{33,17},{49,33},{2,50}... | collective-permute-start | bytes 1572872 | tf_op jit(solution)/shard_map/ppermute | solution.py:204
  164.0 23.3 %collective-permute-start.6 = (bf16[8,2,128,128]{3,2,1,0:T(8,128)(2,1)S(1)}, bf16[8,2,128,128]{3,2,1,0:T(8,128)(2,1)S(1)}, u32[]{:S(2)}, u32[]{:S(2)}) collective-permute-start(bf16[8,2,128,128]{3,2,1,0:T(8,128)(2,1)S(1)} %collective-permute-done.2.refs_2_), channel_id=1, source_target_pairs={{0,16},{16,32},{32,48},{48,0},{1,17},{17,33},{33,49},{49,1},{2,18}... | collective-permute-start | bytes 1572872 | tf_op jit(solution)/shard_map/ppermute | solution.py:204
  164.3 23.9 %collective-permute-start.9 = (bf16[8,2,128,128]{3,2,1,0:T(8,128)(2,1)S(1)}, bf16[8,2,128,128]{3,2,1,0:T(8,128)(2,1)S(1)}, u32[]{:S(2)}, u32[]{:S(2)}) collective-permute-start(bf16[8,2,128,128]{3,2,1,0:T(8,128)(2,1)S(1)} %collective-permute-done.1.refs_1_), channel_id=1, source_target_pairs={{0,8},{8,0},{1,9},{9,1},{2,10},{10,2},{3,11},{11,3},{4,12},{12,4},... | collective-permute-start | bytes 1572872 | tf_op jit(solution)/shard_map/ppermute | solution.py:204
  176.7 11.6 %collective-permute-start.10 = (bf16[8,2,128,128]{3,2,1,0:T(8,128)(2,1)S(1)}, bf16[8,2,128,128]{3,2,1,0:T(8,128)(2,1)S(1)}, u32[]{:S(2)}, u32[]{:S(2)}) collective-permute-start(bf16[8,2,128,128]{3,2,1,0:T(8,128)(2,1)S(1)} %collective-permute-done.2.refs_2_), channel_id=1, source_target_pairs={{0,8},{8,0},{1,9},{9,1},{2,10},{10,2},{3,11},{11,3},{4,12},{12,4},... | collective-permute-start | bytes 1572872 | tf_op jit(solution)/shard_map/ppermute | solution.py:204
  176.7 12.1 %collective-permute-start.12 = (bf16[8,2,128,128]{3,2,1,0:T(8,128)(2,1)S(1)}, bf16[8,2,128,128]{3,2,1,0:T(8,128)(2,1)S(1)}, u32[]{:S(2)}, u32[]{:S(2)}) collective-permute-start(bf16[8,2,128,128]{3,2,1,0:T(8,128)(2,1)S(1)} %collective-permute-done.4.refs_4_), channel_id=1, source_target_pairs={{0,8},{8,0},{1,9},{9,1},{2,10},{10,2},{3,11},{11,3},{4,12},{12,4},... | collective-permute-start | bytes 1572872 | tf_op jit(solution)/shard_map/ppermute | solution.py:204
  187.4 13.3 %collective-permute-start.7 = (bf16[8,2,128,128]{3,2,1,0:T(8,128)(2,1)S(1)}, bf16[8,2,128,128]{3,2,1,0:T(8,128)(2,1)S(1)}, u32[]{:S(2)}, u32[]{:S(2)}) collective-permute-start(bf16[8,2,128,128]{3,2,1,0:T(8,128)(2,1)S(1)} %collective-permute-done.6.refs_6_), channel_id=1, source_target_pairs={{0,64},{64,0},{1,65},{65,1},{2,66},{66,2},{3,67},{67,3},{4,68},{68... | collective-permute-start | bytes 1572872 | tf_op jit(solution)/shard_map/ppermute | solution.py:204
  188.3 18.0 %collective-permute-start.14 = (bf16[8,2,128,128]{3,2,1,0:T(8,128)(2,1)S(1)}, bf16[8,2,128,128]{3,2,1,0:T(8,128)(2,1)S(1)}, u32[]{:S(2)}, u32[]{:S(2)}) collective-permute-start(bf16[8,2,128,128]{3,2,1,0:T(8,128)(2,1)S(1)} %collective-permute-done.6.refs_6_), channel_id=1, source_target_pairs={{0,8},{8,0},{1,9},{9,1},{2,10},{10,2},{3,11},{11,3},{4,12},{12,4},... | collective-permute-start | bytes 1572872 | tf_op jit(solution)/shard_map/ppermute | solution.py:204
  188.3 17.9 %collective-permute-start.11 = (bf16[8,2,128,128]{3,2,1,0:T(8,128)(2,1)S(1)}, bf16[8,2,128,128]{3,2,1,0:T(8,128)(2,1)S(1)}, u32[]{:S(2)}, u32[]{:S(2)}) collective-permute-start(bf16[8,2,128,128]{3,2,1,0:T(8,128)(2,1)S(1)} %collective-permute-done.3.refs_3_), channel_id=1, source_target_pairs={{0,8},{8,0},{1,9},{9,1},{2,10},{10,2},{3,11},{11,3},{4,12},{12,4},... | collective-permute-start | bytes 1572872 | tf_op jit(solution)/shard_map/ppermute | solution.py:204
  188.8 17.5 %collective-permute-start.13 = (bf16[8,2,128,128]{3,2,1,0:T(8,128)(2,1)S(1)}, bf16[8,2,128,128]{3,2,1,0:T(8,128)(2,1)S(1)}, u32[]{:S(2)}, u32[]{:S(2)}) collective-permute-start(bf16[8,2,128,128]{3,2,1,0:T(8,128)(2,1)S(1)} %collective-permute-done.5.refs_5_), channel_id=1, source_target_pairs={{0,8},{8,0},{1,9},{9,1},{2,10},{10,2},{3,11},{11,3},{4,12},{12,4},... | collective-permute-start | bytes 1572872 | tf_op jit(solution)/shard_map/ppermute | solution.py:204
  200.7 5.6 %collective-permute-start.15 = (bf16[8,2,128,128]{3,2,1,0:T(8,128)(2,1)S(1)}, bf16[8,2,128,128]{3,2,1,0:T(8,128)(2,1)S(1)}, u32[]{:S(2)}, u32[]{:S(2)}) collective-permute-start(bf16[8,2,128,128]{3,2,1,0:T(8,128)(2,1)S(1)} %collective-permute-done.7.refs_7_), channel_id=1, source_target_pairs={{0,8},{8,0},{1,9},{9,1},{2,10},{10,2},{3,11},{11,3},{4,12},{12,4},... | collective-permute-start | bytes 1572872 | tf_op jit(solution)/shard_map/ppermute | solution.py:204
